TPU v7x, 32 devices: a whole 2x2x4 slice. The times are simulated.
32 devices in a mesh: groups: 2 (over x), angle: 8 (over z, y), tile: 2 (over core).
Axes of the slice: x: 2, y: 2, z: 4, core: 2. Of those that a mesh axis runs over, the one named last changes fastest.
Arguments:
- intensity: float32 [128, 128, 2048], P(('groups', 'angle', 'tile')), parts along dimension 0, may hold values from 0.2 to 1
- counts: int32 [16], P('groups'), parts along dimension 0, may hold values from 1 to 32, 128 in all
- segment_ids: int32 [64, 64], replicated, may hold values from 0 to 15
- tile_ids: int32 [64, 64], replicated, may hold values from 0 to 15
- block_order: int32 [128], P('groups'), parts along dimension 0, may hold values from 0 to 63, each once
- tiles: bfloat16 [16, 128, 128], replicated, may hold values from -0.0625 to 0.0625
Outputs:
- volume: float32 [16, 32, 64, 128], P(('groups', 'angle'), None, 'tile'), parts along dimension 0
There are 2 independent parts, one for each index of `groups`. A program takes and returns all parts, laid end to end along the dimension named above; an argument that names none is the same for every part. Nothing has to cross between parts.
Inputs may be any that keep to these rules, and one draw needn't show every extreme that they name: Slice group g takes counts[g] consecutive detector rows, groups in order; the counts sum to 128 and the largest is exactly 32. `block_order`: each voxel block appears once.
All inputs are finite; a program needn't handle non-finite values.
Results may differ from a plain program's by a relative error of at most 0.00075.
Values may be sent and summed in bfloat16 or wider, within the bound.
No kernel may reach another device: no remote copies, remote signals or barrier semaphores. Data moves between devices by JAX's collectives and lax.ppermute only.
A program may use at most 128 MiB of HBM per device.

v0:
```python
import functools
import math

import jax
import jax.numpy as jnp
import numpy as np
from jax import lax
from jax.experimental import pallas as pl
from jax.experimental.pallas import tpu as pltpu
from jax.sharding import PartitionSpec as P

paganin_alpha = 2.0
lanes = 128
thickness_bound = 1.75
send_bound = 60000.0


def split_parts(values):
    high = values.astype(jnp.bfloat16)
    low = (values - high.astype(jnp.float32)).astype(jnp.bfloat16)
    return high, low


def split_table(matrix):
    high = matrix.astype(jnp.bfloat16)
    low = (matrix - high.astype(np.float64)).astype(jnp.bfloat16)
    top = np.concatenate([high, high], axis=1)
    bottom = np.concatenate([low, low], axis=1)
    return jnp.asarray(np.concatenate([top, bottom], axis=0))


def filter_tables(row_total, width):
    levels = width.bit_length() - 1
    assert 1 << levels == width
    index = np.arange(row_total)
    phase = 2.0 * np.pi / row_total * (index[:, None] * index[None, :] % row_total)
    hartley = (np.cos(phase) + np.sin(phase)) / math.sqrt(row_total)
    row_weight = 4.0 * np.square(np.sin(np.pi * index / row_total))
    half = (1.0 + paganin_alpha * (row_weight + 2.0)) / (2.0 * paganin_alpha)
    root = half - np.sqrt(half * half - 1.0)
    scale = root / paganin_alpha / np.square(1.0 - root**width)
    factors = np.zeros((row_total, lanes), np.float32)
    for s in range(levels):
        power = root ** (1 << s)
        factors[:, s] = power / (1.0 + power * power)
        scale = scale * (1.0 + power * power)
    return split_table(hartley), split_table(hartley * scale[None, :]), jnp.asarray(factors)


def shifted(values, distance):
    width = values.shape[1]
    if distance % lanes:
        return pltpu.roll(values, distance, 1)
    return jnp.concatenate([values[:, width - distance :], values[:, : width - distance]], axis=1)


def filter_kernel(forward_ref, back_ref, factor_ref, f_ref, out_ref, modes_ref, parts_ref):
    row_total, width = f_ref.shape[1:]
    levels = width.bit_length() - 1
    high, low = split_parts(f_ref[0])
    parts_ref[:row_total] = high
    parts_ref[row_total:] = low
    both = jnp.dot(forward_ref[...], parts_ref[...], preferred_element_type=jnp.float32)
    modes_ref[...] = both[:row_total] + both[row_total:]

    def column_filter(step, carry):
        pieces = []
        for half in range(2):
            rows = pl.ds(pl.multiple_of(step * 16 + half * 8, 8), 8)
            values = modes_ref[rows, :]
            factors = factor_ref[rows, :]
            for s in range(levels):
                distance = 1 << s
                around = shifted(values, distance) + shifted(values, width - distance)
                values = values + factors[:, s : s + 1] * around
            pieces.append(values)
        high, low = split_parts(jnp.concatenate(pieces, axis=0))
        parts_ref[pl.ds(pl.multiple_of(step * 16, 16), 16), :] = high
        parts_ref[pl.ds(pl.multiple_of(row_total + step * 16, 16), 16), :] = low
        return carry

    lax.fori_loop(0, row_total // 16, column_filter, 0)
    both = jnp.dot(back_ref[...], parts_ref[...], preferred_element_type=jnp.float32)
    thickness = (-jnp.log(both[:row_total] + both[row_total:])).astype(jnp.bfloat16)
    edge = out_ref.shape[3]
    for segment in range(width // edge):
        out_ref[0, segment] = thickness[:, segment * edge : (segment + 1) * edge]


def paganin_thickness(intensity, voxel_edge):
    angle_count, row_total, width = intensity.shape
    forward, back, factors = filter_tables(row_total, width)
    segments = width // voxel_edge
    whole = lambda a: (0, 0)
    return pl.pallas_call(
        filter_kernel,
        grid=(angle_count,),
        in_specs=[
            pl.BlockSpec(forward.shape, whole),
            pl.BlockSpec(back.shape, whole),
            pl.BlockSpec(factors.shape, whole),
            pl.BlockSpec((1, row_total, width), lambda a: (a, 0, 0)),
        ],
        out_specs=pl.BlockSpec((1, segments, row_total, voxel_edge), lambda a: (a, 0, 0, 0)),
        out_shape=jax.ShapeDtypeStruct((angle_count, segments, row_total, voxel_edge), jnp.bfloat16),
        scratch_shapes=[
            pltpu.VMEM((row_total, width), jnp.float32),
            pltpu.VMEM((2 * row_total, width), jnp.bfloat16),
        ],
        name="paganin",
    )(forward, back, factors, intensity)


def send_scale(largest, angle_total, voxel_edge):
    limit = send_bound / (angle_total * voxel_edge * thickness_bound)
    scale = jnp.float32(1.0)
    for bits in (32, 16, 8, 4, 2, 1):
        wider = scale * float(2**bits)
        scale = jnp.where(largest * wider <= limit, wider, scale)
    return scale


def backproject_kernel(
    place_ref, counts_ref, segment_ref, tile_ref, order_ref, tiles_ref, *refs
):
    *thickness_refs, out_ref, unscale_ref, rows_ref = refs
    group_total, block_total, capacity, edge = out_ref.shape
    source_total = len(thickness_refs)
    angle_count, _, row_total, _ = thickness_refs[0].shape
    group, tile = place_ref[0], place_ref[1]
    largest = jnp.max(jnp.abs(tiles_ref[...].astype(jnp.float32)))
    scale = send_scale(largest, angle_count * source_total, edge)
    unscale_ref[...] = jnp.full(unscale_ref.shape, 1.0, jnp.float32) / scale
    starts = [jnp.int32(0)]
    for g in range(group_total - 1):
        starts.append(starts[-1] + counts_ref[g])
    rows_ref[:, row_total:] = jnp.zeros((rows_ref.shape[0], capacity, edge), jnp.float32)

    def one_block(block, slot):
        voxel_block = order_ref[tile * block_total + block]
        pieces, matrices = [], []
        for shift, thickness_ref in enumerate(thickness_refs):
            source = lax.rem(tile + source_total - shift, source_total)
            for local in range(angle_count):
                angle = (group * source_total + source) * angle_count + local
                pieces.append(thickness_ref[local, segment_ref[angle, voxel_block]])
                matrices.append(tiles_ref[tile_ref[angle, voxel_block]])
        total = jnp.dot(
            jnp.concatenate(pieces, axis=1),
            jnp.concatenate(matrices, axis=0),
            preferred_element_type=jnp.float32,
        )
        rows_ref[slot, :row_total] = total * scale
        for g in range(group_total):
            out_ref[g, block] = rows_ref[slot, pl.ds(starts[g], capacity), :]

    depth = rows_ref.shape[0]

    def some_blocks(step, carry):
        for slot in range(depth):
            one_block(step * depth + slot, slot)
        return carry

    lax.fori_loop(0, block_total // depth, some_blocks, 0)


def backproject(place, counts, segment_ids, tile_ids, block_order, tiles, thickness, group_total, capacity):
    source_total = len(thickness)
    row_total, edge = thickness[0].shape[2:]
    block_total = block_order.shape[0] // source_total
    depth = 2 if block_total % 2 == 0 else 1
    scalars = pl.BlockSpec(memory_space=pltpu.SMEM)
    vectors = pl.BlockSpec(memory_space=pltpu.VMEM)
    return pl.pallas_call(
        backproject_kernel,
        in_specs=[scalars] * 5 + [vectors] * (1 + source_total),
        out_specs=[vectors, vectors],
        out_shape=[
            jax.ShapeDtypeStruct((group_total, block_total, capacity, edge), jnp.float32),
            jax.ShapeDtypeStruct((8, edge), jnp.float32),
        ],
        scratch_shapes=[pltpu.VMEM((depth, row_total + capacity, edge), jnp.float32)],
        name="backproject",
    )(place, counts, segment_ids, tile_ids, block_order, tiles, *thickness)


def per_device(intensity, counts, segment_ids, tile_ids, block_order, tiles):
    row_total = intensity.shape[1]
    voxel_edge = tiles.shape[1]
    group_total = lax.axis_size("angle")
    tile_total = lax.axis_size("tile")
    capacity = 2 * row_total // group_total
    thickness = paganin_thickness(intensity, voxel_edge)
    sources = [thickness]
    for shift in range(1, tile_total):
        ring = [(i, (i + shift) % tile_total) for i in range(tile_total)]
        sources.append(lax.ppermute(thickness, "tile", ring))
    place = jnp.stack([lax.axis_index("angle"), lax.axis_index("tile")]).astype(jnp.int32)
    partial, unscale = backproject(
        place, counts, segment_ids, tile_ids, block_order, tiles, sources, group_total, capacity
    )
    arrived = lax.all_to_all(partial.astype(jnp.float16), "angle", split_axis=0, concat_axis=0, tiled=True)
    volume = jnp.sum(arrived.astype(jnp.float32), axis=0) * unscale[0, 0]
    slot_valid = jnp.arange(capacity, dtype=jnp.int32) < counts[lax.axis_index("angle")]
    volume = jnp.where(slot_valid[None, :, None], volume, 0.0)
    return jnp.swapaxes(volume, 0, 1)[None]


def solution(mesh):
    in_specs = (P(("groups", "angle", "tile"), None, None), P("groups"), P(), P(), P("groups"), P())
    out_specs = P(("groups", "angle"), None, "tile", None)
    return jax.shard_map(
        per_device, mesh=mesh, in_specs=in_specs, out_specs=out_specs, check_vma=False
    )
```

profile of v0, /device:TPU:0, one launch (start us, length us, event | category | flops | bytes accessed | tf_op | source)
XLA Modules:
  0.0 120.3 jit_solution(10446553563201640270)
XLA Ops:
  0.0 42.9 %paganin.1.refs_0_ = bf16[4,16,128,128]{3,2,1,0:T(8,128)(2,1)} custom-call(bf16[256,256]{1,0:T(8,128)(2,1)} %constant.20.clone.forward_ref, bf16[256,256]{1,0:T(8,128)(2,1)} %constant.21.clone.back_ref, f32[128,128]{1,0:T(8,128)} %constant.22.clone.factor_ref, f32[4,128,2048]{2,1,0:T(8,128)} %f_ref.1), custom_call_target="tpu_custom_call" | custom-call | tf_op jit(solution)/shard_map/paganin/pallas_call | solution.py:95
  42.9 0.5 collective-permute-start
  43.4 0.7 pad_add_fusion.place_ref
  44.1 3.3 %collective-permute-done.refs_1_ = bf16[4,16,128,128]{3,2,1,0:T(8,128)(2,1)S(1)} collective-permute-done((bf16[4,16,128,128]{3,2,1,0:T(8,128)(2,1)}, bf16[4,16,128,128]{3,2,1,0:T(8,128)(2,1)S(1)}, u32[]{:S(2)}, u32[]{:S(2)}) %collective-permute-start) | collective-permute-done | bytes 2097184 | tf_op jit(solution)/shard_map/ppermute | solution.py:197
  47.4 0.0 copy-start
  47.4 1.3 %copy-done = bf16[4,16,128,128]{3,2,1,0:T(8,128)(2,1)} copy-done((bf16[4,16,128,128]{3,2,1,0:T(8,128)(2,1)}, bf16[4,16,128,128]{3,2,1,0:T(8,128)(2,1)S(1)}, u32[]{:S(2)}) %copy-start) | copy-done | bytes 2097176
  48.7 9.5 %backproject.1 = (f32[8,32,32,128]{3,2,1,0:T(8,128)}, f32[8,128]{1,0:T(8,128)}) custom-call(s32[2]{0:T(128)} %pad_add_fusion.place_ref, s32[8]{0:T(128)} %counts_ref.1, s32[64,64]{1,0:T(8,128)} %segment_ref.1, s32[64,64]{1,0:T(8,128)} %tile_ref.1, s32[64]{0:T(128)} %order_ref.1, bf16[16,128,128]{2,1,0:T(8,128)(2,1)} %tiles_ref.1, ...), custom_call_target="tpu_custom_call" | custom-call | tf_op jit(solution)/shard_map/backproject/pallas_call | solution.py:174
  58.3 4.0 %convert_element_type.6 = f16[8,32,32,128]{3,2,1,0:T(8,128)(2,1)} convert(f32[8,32,32,128]{3,2,1,0:T(8,128)} %get-tuple-element.7) | non-fusion elementwise | flops 1048576 | bytes 6291456 | tf_op jit(solution)/shard_map/convert_element_type | solution.py:202
  62.3 0.0 copy-start.1
  62.3 7.3 %all-to-all-start = ((f16[8,32,32,128]{3,2,1,0:T(8,128)(2,1)}), f16[8,32,32,128]{3,2,1,0:T(8,128)(2,1)S(1)}, u32[]{:S(2)}, u32[]{:S(2)}) async-start(f16[8,32,32,128]{3,2,1,0:T(8,128)(2,1)} %convert_element_type.6), calls=%async_computation | async-start | bytes 4194304 | tf_op jit(solution)/shard_map/all_to_all | solution.py:202
  69.6 0.0 copy-done.1
  69.6 0.6 dynamic_slice.3
  70.2 0.6 iota_compare_fusion
  70.8 1.2 %slice.3 = f32[1,1]{1,0:T(1,128)} slice(f32[8,128]{1,0:T(8,128)} %get-tuple-element.8), slice={[0:1], [0:1]} | slice | bytes 8 | tf_op jit(solution)/shard_map/slice | solution.py:203
  72.1 46.1 %all-to-all-done = f16[8,32,32,128]{3,2,1,0:T(8,128)(2,1)S(1)} async-done(((f16[8,32,32,128]{3,2,1,0:T(8,128)(2,1)}), f16[8,32,32,128]{3,2,1,0:T(8,128)(2,1)S(1)}, u32[]{:S(2)}, u32[]{:S(2)}) %all-to-all-start) | async-done | bytes 2097184 | tf_op jit(solution)/shard_map/all_to_all | solution.py:202
  118.1 0.3 convert_reduce_fusion
  118.4 0.7 select_bitcast_fusion
  119.2 1.1 copy.10
Async XLA Ops:
  42.9 4.5 %collective-permute-start = (bf16[4,16,128,128]{3,2,1,0:T(8,128)(2,1)}, bf16[4,16,128,128]{3,2,1,0:T(8,128)(2,1)S(1)}, u32[]{:S(2)}, u32[]{:S(2)}) collective-permute-start(bf16[4,16,128,128]{3,2,1,0:T(8,128)(2,1)} %paganin.1.refs_0_), channel_id=1, source_target_pairs={{0,1},{1,0},{2,3},{3,2},{4,5},{5,4},{6,7},{7,6},{8,9},{9,8},{10,11... | collective-permute-start | bytes 6291464 | tf_op jit(solution)/shard_map/ppermute | solution.py:197
  47.4 1.3 %copy-start = (bf16[4,16,128,128]{3,2,1,0:T(8,128)(2,1)}, bf16[4,16,128,128]{3,2,1,0:T(8,128)(2,1)S(1)}, u32[]{:S(2)}) copy-start(bf16[4,16,128,128]{3,2,1,0:T(8,128)(2,1)S(1)} %collective-permute-done.refs_1_) | copy-start | bytes 6291460
  62.3 7.3 %copy-start.1 = (s32[8]{0:T(128)S(1)}, s32[8]{0:T(128)}, u32[]{:S(2)}) copy-start(s32[8]{0:T(128)} %counts_ref.1) | copy-start | bytes 100
  62.3 55.9 %all-to-all-start = ((f16[8,32,32,128]{3,2,1,0:T(8,128)(2,1)}), f16[8,32,32,128]{3,2,1,0:T(8,128)(2,1)S(1)}, u32[]{:S(2)}, u32[]{:S(2)}) async-start(f16[8,32,32,128]{3,2,1,0:T(8,128)(2,1)} %convert_element_type.6), calls=%async_computation | async-start | bytes 4194304 | tf_op jit(solution)/shard_map/all_to_all | solution.py:202
where the time goes:
time: 121 us; the launch traced here: 120 us
  Pallas kernels  52.4 us (43%)
  waiting for transfers between devices  49.4 us (41%)
  starting transfers between devices  7.81 us (6%)
  other arithmetic  6.29 us (5%)
  local copies, waits for them, and re-layouts  4.3 us (4%)
    all_to_all x1, waiting for transfers between devices, per_device(): lax.all_to_all(partial.astype(jnp.float16), 'angle', split_axis=0, concat...  46.1 us
    pallas_call x1, Pallas kernels, paganin_thickness(): pl.pallas_call(filter_kernel, grid=(angle_count,), in_specs=[pl.BlockSpec...  42.9 us
    pallas_call x1, Pallas kernels, backproject(): pl.pallas_call(backproject_kernel, in_specs=[scalars] * 5 + [vectors] * (...  9.51 us
    all_to_all x1, starting transfers between devices, per_device(): lax.all_to_all(partial.astype(jnp.float16), 'angle', split_axis=0, concat...  7.32 us
    convert_element_type x1, other arithmetic, per_device(): partial.astype(jnp.float16)  4.01 us
    ppermute x1, waiting for transfers between devices, per_device(): sources.append(lax.ppermute(thickness, 'tile', ring))  3.35 us
  transfers between devices with their start and end apart: 2, of which 2 were waited for; matrix products, arithmetic and copies ran while one was open for 3% of the time, Pallas kernels for 0%

commit v1 on v0

--- a/solution.py
+++ b/solution.py
@@ -11,6 +11,10 @@
 
 paganin_alpha = 2.0
 lanes = 128
+sublanes = 8
+strands = 8
+chunks = strands * sublanes
+pitch_pad = 8
 thickness_bound = 1.75
 send_bound = 60000.0
 
@@ -21,75 +25,101 @@
     return high, low
 
 
-def split_table(matrix):
+def paired_parts(values):
+    high, low = split_parts(values)
+    return jnp.concatenate([high, low, high], axis=1)
+
+
+def paired_table(matrix, axis):
     high = matrix.astype(jnp.bfloat16)
     low = (matrix - high.astype(np.float64)).astype(jnp.bfloat16)
-    top = np.concatenate([high, high], axis=1)
-    bottom = np.concatenate([low, low], axis=1)
-    return jnp.asarray(np.concatenate([top, bottom], axis=0))
-
-
-def filter_tables(row_total, width):
-    levels = width.bit_length() - 1
-    assert 1 << levels == width
+    return jnp.asarray(np.concatenate([high, high, low], axis=axis))
+
+
+def filter_tables(row_total, chunk):
     index = np.arange(row_total)
     phase = 2.0 * np.pi / row_total * (index[:, None] * index[None, :] % row_total)
     hartley = (np.cos(phase) + np.sin(phase)) / math.sqrt(row_total)
     row_weight = 4.0 * np.square(np.sin(np.pi * index / row_total))
     half = (1.0 + paganin_alpha * (row_weight + 2.0)) / (2.0 * paganin_alpha)
     root = half - np.sqrt(half * half - 1.0)
-    scale = root / paganin_alpha / np.square(1.0 - root**width)
-    factors = np.zeros((row_total, lanes), np.float32)
+    levels = chunks.bit_length() - 1
+    powers = [root] + [root ** (chunk << s) for s in range(levels)]
+    powers.append(1.0 / (1.0 - root ** (chunk * chunks)))
+    powers = np.repeat(np.stack(powers), sublanes, axis=0).astype(np.float32)
+    back = hartley * (root / paganin_alpha)[None, :]
+    return paired_table(hartley, 0), paired_table(back, 1), jnp.asarray(powers)
+
+
+def chunk_shift(values, distance):
+    moved = []
+    for q in range(strands):
+        turns, source = divmod(q - distance, strands)
+        moved.append(pltpu.roll(values[source], -turns % sublanes, 0) if turns % sublanes else values[source])
+    return moved
+
+
+def carries(ends, powers_ref, direction):
+    levels = chunks.bit_length() - 1
     for s in range(levels):
-        power = root ** (1 << s)
-        factors[:, s] = power / (1.0 + power * power)
-        scale = scale * (1.0 + power * power)
-    return split_table(hartley), split_table(hartley * scale[None, :]), jnp.asarray(factors)
-
-
-def shifted(values, distance):
-    width = values.shape[1]
-    if distance % lanes:
-        return pltpu.roll(values, distance, 1)
-    return jnp.concatenate([values[:, width - distance :], values[:, : width - distance]], axis=1)
-
-
-def filter_kernel(forward_ref, back_ref, factor_ref, f_ref, out_ref, modes_ref, parts_ref):
+        power = powers_ref[pl.ds((1 + s) * sublanes, sublanes), :]
+        before = chunk_shift(ends, direction << s)
+        ends = [end + power * other for end, other in zip(ends, before)]
+    whole = powers_ref[pl.ds((1 + levels) * sublanes, sublanes), :]
+    return [whole * other for other in chunk_shift(ends, direction)]
+
+
+def filter_kernel(forward_ref, back_ref, powers_ref, f_ref, out_ref, modes_ref):
     row_total, width = f_ref.shape[1:]
-    levels = width.bit_length() - 1
-    high, low = split_parts(f_ref[0])
-    parts_ref[:row_total] = high
-    parts_ref[row_total:] = low
-    both = jnp.dot(forward_ref[...], parts_ref[...], preferred_element_type=jnp.float32)
-    modes_ref[...] = both[:row_total] + both[row_total:]
-
-    def column_filter(step, carry):
-        pieces = []
-        for half in range(2):
-            rows = pl.ds(pl.multiple_of(step * 16 + half * 8, 8), 8)
-            values = modes_ref[rows, :]
-            factors = factor_ref[rows, :]
-            for s in range(levels):
-                distance = 1 << s
-                around = shifted(values, distance) + shifted(values, width - distance)
-                values = values + factors[:, s : s + 1] * around
-            pieces.append(values)
-        high, low = split_parts(jnp.concatenate(pieces, axis=0))
-        parts_ref[pl.ds(pl.multiple_of(step * 16, 16), 16), :] = high
-        parts_ref[pl.ds(pl.multiple_of(row_total + step * 16, 16), 16), :] = low
-        return carry
-
-    lax.fori_loop(0, row_total // 16, column_filter, 0)
-    both = jnp.dot(back_ref[...], parts_ref[...], preferred_element_type=jnp.float32)
-    thickness = (-jnp.log(both[:row_total] + both[row_total:])).astype(jnp.bfloat16)
     edge = out_ref.shape[3]
-    for segment in range(width // edge):
-        out_ref[0, segment] = thickness[:, segment * edge : (segment + 1) * edge]
+    span = width // sublanes
+    pitch = modes_ref.shape[0] // sublanes
+    chunk = span // strands
+
+    def place(column):
+        return column // span * pitch + column % span
+
+    for column in range(0, width, lanes):
+        turned = f_ref[0, :, column : column + lanes].T
+        modes_ref[pl.ds(place(column), lanes), :] = jnp.dot(
+            paired_parts(turned), forward_ref[...], preferred_element_type=jnp.float32
+        )
+
+    root = powers_ref[pl.ds(0, sublanes), :]
+
+    def strand(q, step):
+        return pl.ds(q * chunk + step, sublanes, stride=pitch)
+
+    def sweep(values, order, keep):
+        for step in order:
+            for q in range(strands):
+                values[q] = modes_ref[strand(q, step), :] + root * values[q]
+                if keep:
+                    modes_ref[strand(q, step), :] = values[q]
+        return values
+
+    for direction in (1, -1):
+        order = range(chunk)[::direction]
+        zeros = [jnp.zeros((sublanes, row_total), jnp.float32)] * strands
+        ends = sweep(zeros, order, False)
+        sweep(carries(ends, powers_ref, direction), order, True)
+
+    for column in range(0, width, lanes):
+        filtered = lax.dot_general(
+            back_ref[...],
+            paired_parts(modes_ref[pl.ds(place(column), lanes), :]),
+            (((1,), (1,)), ((), ())),
+            preferred_element_type=jnp.float32,
+        )
+        thickness = (-jnp.log(filtered)).astype(jnp.bfloat16)
+        for part in range(lanes // edge):
+            out_ref[0, column // edge + part] = thickness[:, part * edge : (part + 1) * edge]
 
 
 def paganin_thickness(intensity, voxel_edge):
     angle_count, row_total, width = intensity.shape
-    forward, back, factors = filter_tables(row_total, width)
+    assert row_total == lanes and width % (sublanes * lanes) == 0 and lanes % voxel_edge == 0
+    forward, back, powers = filter_tables(row_total, width // chunks)
     segments = width // voxel_edge
     whole = lambda a: (0, 0)
     return pl.pallas_call(
@@ -98,17 +128,14 @@
         in_specs=[
             pl.BlockSpec(forward.shape, whole),
             pl.BlockSpec(back.shape, whole),
-            pl.BlockSpec(factors.shape, whole),
+            pl.BlockSpec(powers.shape, whole),
             pl.BlockSpec((1, row_total, width), lambda a: (a, 0, 0)),
         ],
         out_specs=pl.BlockSpec((1, segments, row_total, voxel_edge), lambda a: (a, 0, 0, 0)),
         out_shape=jax.ShapeDtypeStruct((angle_count, segments, row_total, voxel_edge), jnp.bfloat16),
-        scratch_shapes=[
-            pltpu.VMEM((row_total, width), jnp.float32),
-            pltpu.VMEM((2 * row_total, width), jnp.bfloat16),
-        ],
+        scratch_shapes=[pltpu.VMEM((width + sublanes * pitch_pad, row_total), jnp.float32)],
         name="paganin",
-    )(forward, back, factors, intensity)
+    )(forward, back, powers, intensity)
 
 
 def send_scale(largest, angle_total, voxel_edge):

time: 121 us -> 88.7 us (0.73)
  Pallas kernels: 52.4 us -> 20.5 us
    pallas_call x1, Pallas kernels: 42.9 us -> 11 us  [paganin_thickness(): pl.pallas_call(filter_kernel, grid=(angle_count,), in_specs=[pl.BlockSpec...]
  transfers between devices with their start and end apart: 2 -> 2, of which waited for: 2 -> 2; matrix products, arithmetic and copies ran while one was open for 3% -> 4% of each run, Pallas kernels for 0% -> 0%
where the time goes in v1:
time: 88.7 us; the launch traced here: 88.4 us
  waiting for transfers between devices  49.4 us (56%)
  Pallas kernels  20.5 us (23%)
  starting transfers between devices  7.81 us (9%)
  other arithmetic  6.29 us (7%)
  local copies, waits for them, and re-layouts  4.3 us (5%)
    all_to_all x1, waiting for transfers between devices, per_device(): lax.all_to_all(partial.astype(jnp.float16), 'angle', split_axis=0, concat...  46.1 us
    pallas_call x1, Pallas kernels, paganin_thickness(): pl.pallas_call(filter_kernel, grid=(angle_count,), in_specs=[pl.BlockSpec...  11 us
    pallas_call x1, Pallas kernels, backproject(): pl.pallas_call(backproject_kernel, in_specs=[scalars] * 5 + [vectors] * (...  9.5 us
    all_to_all x1, starting transfers between devices, per_device(): lax.all_to_all(partial.astype(jnp.float16), 'angle', split_axis=0, concat...  7.31 us
    convert_element_type x1, other arithmetic, per_device(): partial.astype(jnp.float16)  4.01 us
    ppermute x1, waiting for transfers between devices, per_device(): sources.append(lax.ppermute(thickness, 'tile', ring))  3.35 us
  transfers between devices with their start and end apart: 2, of which 2 were waited for; matrix products, arithmetic and copies ran while one was open for 4% of the time, Pallas kernels for 0%

profile of v1, /device:TPU:0, one launch (start us, length us, event | category | flops | bytes accessed | tf_op | source)
XLA Modules:
  0.0 88.4 jit_solution(13313726125084181726)
XLA Ops:
  0.0 11.0 %paganin.1.refs_0_ = bf16[4,16,128,128]{3,2,1,0:T(8,128)(2,1)} custom-call(bf16[384,128]{1,0:T(8,128)(2,1)} %constant.20.clone.forward_ref, bf16[128,384]{1,0:T(8,128)(2,1)} %constant.21.clone.back_ref, f32[64,128]{1,0:T(8,128)} %constant.22.clone.powers_ref, f32[4,128,2048]{2,1,0:T(8,128)} %f_ref.1), custom_call_target="tpu_custom_call" | custom-call | tf_op jit(solution)/shard_map/paganin/pallas_call | solution.py:125
  11.0 0.5 collective-permute-start
  11.5 0.7 pad_add_fusion.place_ref
  12.2 3.3 %collective-permute-done.refs_1_ = bf16[4,16,128,128]{3,2,1,0:T(8,128)(2,1)S(1)} collective-permute-done((bf16[4,16,128,128]{3,2,1,0:T(8,128)(2,1)}, bf16[4,16,128,128]{3,2,1,0:T(8,128)(2,1)S(1)}, u32[]{:S(2)}, u32[]{:S(2)}) %collective-permute-start) | collective-permute-done | bytes 2097184 | tf_op jit(solution)/shard_map/ppermute | solution.py:224
  15.5 0.0 copy-start
  15.5 1.3 %copy-done = bf16[4,16,128,128]{3,2,1,0:T(8,128)(2,1)} copy-done((bf16[4,16,128,128]{3,2,1,0:T(8,128)(2,1)}, bf16[4,16,128,128]{3,2,1,0:T(8,128)(2,1)S(1)}, u32[]{:S(2)}) %copy-start) | copy-done | bytes 2097176
  16.9 9.5 %backproject.1 = (f32[8,32,32,128]{3,2,1,0:T(8,128)}, f32[8,128]{1,0:T(8,128)}) custom-call(s32[2]{0:T(128)} %pad_add_fusion.place_ref, s32[8]{0:T(128)} %counts_ref.1, s32[64,64]{1,0:T(8,128)} %segment_ref.1, s32[64,64]{1,0:T(8,128)} %tile_ref.1, s32[64]{0:T(128)} %order_ref.1, bf16[16,128,128]{2,1,0:T(8,128)(2,1)} %tiles_ref.1, ...), custom_call_target="tpu_custom_call" | custom-call | tf_op jit(solution)/shard_map/backproject/pallas_call | solution.py:201
  26.4 4.0 %convert_element_type.6 = f16[8,32,32,128]{3,2,1,0:T(8,128)(2,1)} convert(f32[8,32,32,128]{3,2,1,0:T(8,128)} %get-tuple-element.7) | non-fusion elementwise | flops 1048576 | bytes 6291456 | tf_op jit(solution)/shard_map/convert_element_type | solution.py:229
  30.4 0.0 copy-start.1
  30.4 7.3 %all-to-all-start = ((f16[8,32,32,128]{3,2,1,0:T(8,128)(2,1)}), f16[8,32,32,128]{3,2,1,0:T(8,128)(2,1)S(1)}, u32[]{:S(2)}, u32[]{:S(2)}) async-start(f16[8,32,32,128]{3,2,1,0:T(8,128)(2,1)} %convert_element_type.6), calls=%async_computation | async-start | bytes 4194304 | tf_op jit(solution)/shard_map/all_to_all | solution.py:229
  37.7 0.0 copy-done.1
  37.7 0.6 dynamic_slice.3
  38.3 0.6 iota_compare_fusion
  38.9 1.2 %slice.3 = f32[1,1]{1,0:T(1,128)} slice(f32[8,128]{1,0:T(8,128)} %get-tuple-element.8), slice={[0:1], [0:1]} | slice | bytes 8 | tf_op jit(solution)/shard_map/slice | solution.py:230
  40.2 46.1 %all-to-all-done = f16[8,32,32,128]{3,2,1,0:T(8,128)(2,1)S(1)} async-done(((f16[8,32,32,128]{3,2,1,0:T(8,128)(2,1)}), f16[8,32,32,128]{3,2,1,0:T(8,128)(2,1)S(1)}, u32[]{:S(2)}, u32[]{:S(2)}) %all-to-all-start) | async-done | bytes 2097184 | tf_op jit(solution)/shard_map/all_to_all | solution.py:229
  86.2 0.3 convert_reduce_fusion
  86.5 0.7 select_bitcast_fusion
  87.3 1.1 %copy.10 = f32[1,32,32,128]{3,2,1,0:T(8,128)} copy(f32[1,32,32,128]{3,1,2,0:T(8,128)S(1)} %select_bitcast_fusion) | data formatting | bytes 1048576 | tf_op jit(solution)/shard_map/broadcast_in_dim | solution.py:233
Async XLA Ops:
  11.0 4.5 %collective-permute-start = (bf16[4,16,128,128]{3,2,1,0:T(8,128)(2,1)}, bf16[4,16,128,128]{3,2,1,0:T(8,128)(2,1)S(1)}, u32[]{:S(2)}, u32[]{:S(2)}) collective-permute-start(bf16[4,16,128,128]{3,2,1,0:T(8,128)(2,1)} %paganin.1.refs_0_), channel_id=1, source_target_pairs={{0,1},{1,0},{2,3},{3,2},{4,5},{5,4},{6,7},{7,6},{8,9},{9,8},{10,11... | collective-permute-start | bytes 6291464 | tf_op jit(solution)/shard_map/ppermute | solution.py:224
  15.5 1.3 %copy-start = (bf16[4,16,128,128]{3,2,1,0:T(8,128)(2,1)}, bf16[4,16,128,128]{3,2,1,0:T(8,128)(2,1)S(1)}, u32[]{:S(2)}) copy-start(bf16[4,16,128,128]{3,2,1,0:T(8,128)(2,1)S(1)} %collective-permute-done.refs_1_) | copy-start | bytes 6291460
  30.4 7.3 %copy-start.1 = (s32[8]{0:T(128)S(1)}, s32[8]{0:T(128)}, u32[]{:S(2)}) copy-start(s32[8]{0:T(128)} %counts_ref.1) | copy-start | bytes 100
  30.4 55.9 %all-to-all-start = ((f16[8,32,32,128]{3,2,1,0:T(8,128)(2,1)}), f16[8,32,32,128]{3,2,1,0:T(8,128)(2,1)S(1)}, u32[]{:S(2)}, u32[]{:S(2)}) async-start(f16[8,32,32,128]{3,2,1,0:T(8,128)(2,1)} %convert_element_type.6), calls=%async_computation | async-start | bytes 4194304 | tf_op jit(solution)/shard_map/all_to_all | solution.py:229

commit v2 on v1

--- a/solution.py
+++ b/solution.py
@@ -148,67 +148,82 @@
 
 
 def backproject_kernel(
-    place_ref, counts_ref, segment_ref, tile_ref, order_ref, tiles_ref, *refs
+    partners, place_ref, segment_ref, tile_ref, order_ref, tiles_ref, *refs
 ):
-    *thickness_refs, out_ref, unscale_ref, rows_ref = refs
-    group_total, block_total, capacity, edge = out_ref.shape
+    *thickness_refs, out_ref, unscale_ref = refs
+    chunk_total, share, row_total, edge = out_ref.shape
     source_total = len(thickness_refs)
-    angle_count, _, row_total, _ = thickness_refs[0].shape
-    group, tile = place_ref[0], place_ref[1]
+    angle_count = thickness_refs[0].shape[0]
+    group, tile, group_total = place_ref[0], place_ref[1], place_ref[2]
     largest = jnp.max(jnp.abs(tiles_ref[...].astype(jnp.float32)))
     scale = send_scale(largest, angle_count * source_total, edge)
     unscale_ref[...] = jnp.full(unscale_ref.shape, 1.0, jnp.float32) / scale
-    starts = [jnp.int32(0)]
-    for g in range(group_total - 1):
-        starts.append(starts[-1] + counts_ref[g])
-    rows_ref[:, row_total:] = jnp.zeros((rows_ref.shape[0], capacity, edge), jnp.float32)
-
-    def one_block(block, slot):
-        voxel_block = order_ref[tile * block_total + block]
-        pieces, matrices = [], []
-        for shift, thickness_ref in enumerate(thickness_refs):
-            source = lax.rem(tile + source_total - shift, source_total)
-            for local in range(angle_count):
-                angle = (group * source_total + source) * angle_count + local
-                pieces.append(thickness_ref[local, segment_ref[angle, voxel_block]])
-                matrices.append(tiles_ref[tile_ref[angle, voxel_block]])
-        total = jnp.dot(
-            jnp.concatenate(pieces, axis=1),
-            jnp.concatenate(matrices, axis=0),
-            preferred_element_type=jnp.float32,
-        )
-        rows_ref[slot, :row_total] = total * scale
-        for g in range(group_total):
-            out_ref[g, block] = rows_ref[slot, pl.ds(starts[g], capacity), :]
-
-    depth = rows_ref.shape[0]
-
-    def some_blocks(step, carry):
-        for slot in range(depth):
-            one_block(step * depth + slot, slot)
-        return carry
-
-    lax.fori_loop(0, block_total // depth, some_blocks, 0)
-
-
-def backproject(place, counts, segment_ids, tile_ids, block_order, tiles, thickness, group_total, capacity):
-    source_total = len(thickness)
+
+    for chunk, partner in enumerate(partners):
+        owner = lax.bitwise_xor(group, jnp.int32(partner))
+        for block in range(share):
+            voxel_block = order_ref[(tile * group_total + owner) * share + block]
+            pieces, matrices = [], []
+            for shift, thickness_ref in enumerate(thickness_refs):
+                source = lax.rem(tile + source_total - shift, source_total)
+                for local in range(angle_count):
+                    angle = (group * source_total + source) * angle_count + local
+                    pieces.append(thickness_ref[local, segment_ref[angle, voxel_block]])
+                    matrices.append(tiles_ref[tile_ref[angle, voxel_block]])
+            total = jnp.dot(
+                jnp.concatenate(pieces, axis=1),
+                jnp.concatenate(matrices, axis=0),
+                preferred_element_type=jnp.float32,
+            )
+            out_ref[chunk, block] = total * scale
+
+
+def backproject(partners, place, segment_ids, tile_ids, block_order, tiles, thickness, share):
     row_total, edge = thickness[0].shape[2:]
-    block_total = block_order.shape[0] // source_total
-    depth = 2 if block_total % 2 == 0 else 1
+    angle_total = thickness[0].shape[0] * len(thickness)
+    blocks = len(partners) * share
     scalars = pl.BlockSpec(memory_space=pltpu.SMEM)
     vectors = pl.BlockSpec(memory_space=pltpu.VMEM)
     return pl.pallas_call(
-        backproject_kernel,
-        in_specs=[scalars] * 5 + [vectors] * (1 + source_total),
+        functools.partial(backproject_kernel, tuple(partners)),
+        in_specs=[scalars] * 4 + [vectors] * (1 + len(thickness)),
         out_specs=[vectors, vectors],
         out_shape=[
-            jax.ShapeDtypeStruct((group_total, block_total, capacity, edge), jnp.float32),
+            jax.ShapeDtypeStruct((len(partners), share, row_total, edge), jnp.float32),
             jax.ShapeDtypeStruct((8, edge), jnp.float32),
         ],
-        scratch_shapes=[pltpu.VMEM((depth, row_total + capacity, edge), jnp.float32)],
+        cost_estimate=pl.CostEstimate(
+            flops=2 * blocks * angle_total * row_total * edge * edge,
+            bytes_accessed=4 * blocks * row_total * edge,
+            transcendentals=0,
+        ),
         name="backproject",
-    )(place, counts, segment_ids, tile_ids, block_order, tiles, *thickness)
+    )(place, segment_ids, tile_ids, block_order, tiles, *thickness)
+
+
+def regroup_kernel(counts_ref, rows_ref, out_ref, padded_ref):
+    group_total, share, capacity, edge = out_ref.shape
+    row_total = rows_ref.shape[1]
+    for block in range(share):
+        padded_ref[block, :row_total] = rows_ref[block]
+        padded_ref[block, row_total:] = jnp.zeros((capacity, edge), jnp.float32)
+    start = 0
+    for g in range(group_total):
+        for block in range(share):
+            out_ref[g, block] = padded_ref[block, pl.ds(start, capacity), :]
+        start = start + counts_ref[g]
+
+
+def regroup(counts, rows, group_total, capacity):
+    share, row_total, edge = rows.shape
+    return pl.pallas_call(
+        regroup_kernel,
+        in_specs=[pl.BlockSpec(memory_space=pltpu.SMEM), pl.BlockSpec(memory_space=pltpu.VMEM)],
+        out_specs=pl.BlockSpec(memory_space=pltpu.VMEM),
+        out_shape=jax.ShapeDtypeStruct((group_total, share, capacity, edge), jnp.float32),
+        scratch_shapes=[pltpu.VMEM((share, row_total + capacity, edge), jnp.float32)],
+        name="regroup",
+    )(counts, rows)
 
 
 def per_device(intensity, counts, segment_ids, tile_ids, block_order, tiles):
@@ -216,19 +231,36 @@
     voxel_edge = tiles.shape[1]
     group_total = lax.axis_size("angle")
     tile_total = lax.axis_size("tile")
+    group = lax.axis_index("angle")
     capacity = 2 * row_total // group_total
+    share = block_order.shape[0] // (tile_total * group_total)
+    assert group_total & (group_total - 1) == 0
     thickness = paganin_thickness(intensity, voxel_edge)
     sources = [thickness]
     for shift in range(1, tile_total):
         ring = [(i, (i + shift) % tile_total) for i in range(tile_total)]
         sources.append(lax.ppermute(thickness, "tile", ring))
-    place = jnp.stack([lax.axis_index("angle"), lax.axis_index("tile")]).astype(jnp.int32)
-    partial, unscale = backproject(
-        place, counts, segment_ids, tile_ids, block_order, tiles, sources, group_total, capacity
-    )
-    arrived = lax.all_to_all(partial.astype(jnp.float16), "angle", split_axis=0, concat_axis=0, tiled=True)
-    volume = jnp.sum(arrived.astype(jnp.float32), axis=0) * unscale[0, 0]
-    slot_valid = jnp.arange(capacity, dtype=jnp.int32) < counts[lax.axis_index("angle")]
+    place = jnp.stack([group, lax.axis_index("tile"), jnp.int32(group_total)]).astype(jnp.int32)
+    tables = (place, segment_ids, tile_ids, block_order, tiles, sources, share)
+    half = max(1, group_total // 2)
+    far, unscale = backproject(range(half, group_total)[::-1], *tables)
+    parts = []
+    for partner, partial in zip(range(half, group_total)[::-1], far):
+        swap = [(i, i ^ partner) for i in range(group_total)]
+        parts.append(lax.ppermute(partial.astype(jnp.float16), "angle", swap))
+    near, _ = backproject(range(half)[::-1], *tables)
+    for partner, partial in zip(range(half)[::-1], near):
+        swap = [(i, i ^ partner) for i in range(group_total)]
+        if partner:
+            parts.append(lax.ppermute(partial.astype(jnp.float16), "angle", swap))
+    rows = near[half - 1]
+    for part in parts:
+        rows = rows + part.astype(jnp.float32)
+    slots = regroup(counts, rows, group_total, capacity) * (1.0 / group_total)
+    arrived = lax.all_to_all(slots.astype(jnp.float16), "angle", split_axis=0, concat_axis=0, tiled=True)
+    arrived = arrived.reshape(group_total * share, capacity, voxel_edge)
+    volume = arrived.astype(jnp.float32) * (unscale[0, 0] * group_total)
+    slot_valid = jnp.arange(capacity, dtype=jnp.int32) < counts[group]
     volume = jnp.where(slot_valid[None, :, None], volume, 0.0)
     return jnp.swapaxes(volume, 0, 1)[None]
 

time: 88.7 us -> 72.2 us (0.81)
  waiting for transfers between devices: 49.4 us -> 14.8 us
  starting transfers between devices: 7.81 us -> 22 us
  other arithmetic: 6.29 us -> 8.67 us
  Pallas kernels: 20.5 us -> 22.1 us
  local copies, waits for them, and re-layouts: 4.3 us -> 3.32 us
    all_to_all x1, waiting for transfers between devices: 46.1 us -> 5.12 us  [per_device(): lax.all_to_all(slots.astype(jnp.float16), 'angle', split_axis=0, concat_a...]
    ppermute x0 -> x7, starting transfers between devices: none -> 17.6 us  [per_device(): parts.append(lax.ppermute(partial.astype(jnp.float16), 'angle', swap))]
    ppermute x0 -> x7, waiting for transfers between devices: none -> 6.27 us  [per_device(): parts.append(lax.ppermute(partial.astype(jnp.float16), 'angle', swap))]
    all_to_all x1, starting transfers between devices: 7.31 us -> 3.95 us  [per_device(): lax.all_to_all(slots.astype(jnp.float16), 'angle', split_axis=0, concat_a...]
    another operation x1 -> x3, other arithmetic: 0.65 us -> 3.24 us  [per_device(): jnp.stack([lax.axis_index('angle'), lax.axis_index('tile')])]
    convert_element_type x1, other arithmetic: 4.01 us -> 1.8 us  [per_device(): slots.astype(jnp.float16)]
    add x0 -> x1, other arithmetic: none -> 1.79 us  [per_device(): rows = rows + part.astype(jnp.float32)]
    pallas_call x1 -> x3, Pallas kernels: 9.5 us -> 11.1 us  [the longest x2 9.27 us: backproject(): pl.pallas_call(functools.partial(backproject_kernel, tuple(partners)), in...]
  transfers between devices with their start and end apart: 2 -> 9, of which waited for: 2 -> 5; matrix products, arithmetic and copies ran while one was open for 4% -> 6% of each run, Pallas kernels for 0% -> 6%
where the time goes in v2:
time: 72.2 us; the launch traced here: 71.7 us
  Pallas kernels  22.1 us (31%)
  starting transfers between devices  22 us (30%)
  waiting for transfers between devices  14.8 us (20%)
  other arithmetic  8.67 us (12%)
  local copies, waits for them, and re-layouts  3.32 us (5%)
  between operations  0.73 us (1%)
    ppermute x7, starting transfers between devices, per_device(): parts.append(lax.ppermute(partial.astype(jnp.float16), 'angle', swap))  17.6 us
    pallas_call x1, Pallas kernels, paganin_thickness(): pl.pallas_call(filter_kernel, grid=(angle_count,), in_specs=[pl.BlockSpec...  11.1 us
    pallas_call x2, Pallas kernels, backproject(): pl.pallas_call(functools.partial(backproject_kernel, tuple(partners)), in...  9.27 us
    ppermute x7, waiting for transfers between devices, per_device(): parts.append(lax.ppermute(partial.astype(jnp.float16), 'angle', swap))  6.27 us
    all_to_all x1, waiting for transfers between devices, per_device(): lax.all_to_all(slots.astype(jnp.float16), 'angle', split_axis=0, concat_a...  5.12 us
    all_to_all x1, starting transfers between devices, per_device(): lax.all_to_all(slots.astype(jnp.float16), 'angle', split_axis=0, concat_a...  3.95 us
    ppermute x1, waiting for transfers between devices, per_device(): sources.append(lax.ppermute(thickness, 'tile', ring))  3.4 us
    another operation x2, other arithmetic  2.65 us
  transfers between devices with their start and end apart: 9, of which 5 were waited for; matrix products, arithmetic and copies ran while one was open for 6% of the time, Pallas kernels for 6%

profile of v2, /device:TPU:0, one launch (start us, length us, event | category | flops | bytes accessed | tf_op | source)
XLA Modules:
  0.0 71.7 jit_solution(1862509612369347257)
XLA Ops:
  0.0 11.1 %paganin.1.refs_0_ = bf16[4,16,128,128]{3,2,1,0:T(8,128)(2,1)} custom-call(bf16[384,128]{1,0:T(8,128)(2,1)} %constant.27.clone.forward_ref, bf16[128,384]{1,0:T(8,128)(2,1)} %constant.28.clone.back_ref, f32[64,128]{1,0:T(8,128)} %constant.29.clone.powers_ref, f32[4,128,2048]{2,1,0:T(8,128)} %f_ref.1), custom_call_target="tpu_custom_call" | custom-call | tf_op jit(solution)/shard_map/paganin/pallas_call | solution.py:125
  11.1 0.5 collective-permute-start
  11.6 0.6 pad_add_fusion.place_ref
  12.2 3.4 %collective-permute-done.refs_1_ = bf16[4,16,128,128]{3,2,1,0:T(8,128)(2,1)S(1)} collective-permute-done((bf16[4,16,128,128]{3,2,1,0:T(8,128)(2,1)}, bf16[4,16,128,128]{3,2,1,0:T(8,128)(2,1)S(1)}, u32[]{:S(2)}, u32[]{:S(2)}) %collective-permute-start) | collective-permute-done | bytes 2097184 | tf_op jit(solution)/shard_map/ppermute | solution.py:242
  15.6 1.3 %copy-done = bf16[4,16,128,128]{3,2,1,0:T(8,128)(2,1)} copy-done((bf16[4,16,128,128]{3,2,1,0:T(8,128)(2,1)}, bf16[4,16,128,128]{3,2,1,0:T(8,128)(2,1)S(1)}, u32[]{:S(2)}) %copy-start) | copy-done | bytes 2097176
  16.9 4.6 %backproject.3 = (f32[4,4,128,128]{3,2,1,0:T(8,128)}, f32[8,128]{1,0:T(8,128)}) custom-call(s32[3]{0:T(128)} %pad_add_fusion.place_ref, s32[64,64]{1,0:T(8,128)} %segment_ref.3, s32[64,64]{1,0:T(8,128)} %tile_ref.3, s32[64]{0:T(128)} %order_ref.3, bf16[16,128,128]{2,1,0:T(8,128)(2,1)} %tiles_ref.3, bf16[4,16,128,128]{3,2,1,0:T(8,128)(2,1)} %paganin.1.refs_0_, ...), custom_call_target="tpu_custom_call" | custom-call | flops 536870912 | bytes 1048576 | tf_op jit(solution)/shard_map/backproject/pallas_call | solution.py:187
  21.5 1.3 %convert.11 = f16[4,4,128,128]{3,2,1,0:T(8,128)(2,1)S(1)} convert(f32[4,4,128,128]{3,2,1,0:T(8,128)} %get-tuple-element.9) | non-fusion elementwise | flops 262144 | bytes 1572864 | tf_op jit(solution)/shard_map/convert.6
  22.8 0.1 slice_bitcast_fusion.6
  23.0 6.0 %collective-permute-start.1 = (f16[4,128,128]{2,1,0:T(8,128)(2,1)S(1)}, f16[4,128,128]{2,1,0:T(8,128)(2,1)S(1)}, u32[]{:S(2)}, u32[]{:S(2)}) collective-permute-start(f16[4,128,128]{2,1,0:T(8,128)(2,1)S(1)} %get-tuple-element.11), channel_id=1, source_target_pairs={{0,14},{2,12},{4,10},{6,8},{8,6},{10,4},{12,2},{14,0},{1,15},{3,13... | collective-permute-start | bytes 393224 | tf_op jit(solution)/shard_map/ppermute | solution.py:250
  29.0 0.2 collective-permute-start.2
  29.2 0.7 %collective-permute-start.3 = (f16[4,128,128]{2,1,0:T(8,128)(2,1)S(1)}, f16[4,128,128]{2,1,0:T(8,128)(2,1)S(1)}, u32[]{:S(2)}, u32[]{:S(2)}) collective-permute-start(f16[4,128,128]{2,1,0:T(8,128)(2,1)S(1)} %get-tuple-element.13), channel_id=1, source_target_pairs={{0,10},{2,8},{4,14},{6,12},{8,2},{10,0},{12,6},{14,4},{1,11},{3,9}... | collective-permute-start | bytes 393224 | tf_op jit(solution)/shard_map/ppermute | solution.py:250
  29.9 2.0 %collective-permute-start.4 = (f16[4,128,128]{2,1,0:T(8,128)(2,1)S(1)}, f16[4,128,128]{2,1,0:T(8,128)(2,1)S(1)}, u32[]{:S(2)}, u32[]{:S(2)}) collective-permute-start(f16[4,128,128]{2,1,0:T(8,128)(2,1)S(1)} %get-tuple-element.12), channel_id=1, source_target_pairs={{0,8},{2,10},{4,12},{6,14},{8,0},{10,2},{12,4},{14,6},{1,9},{3,11}... | collective-permute-start | bytes 393224 | tf_op jit(solution)/shard_map/ppermute | solution.py:250
  32.0 4.6 %backproject.2 = (f32[4,4,128,128]{3,2,1,0:T(8,128)}, f32[8,128]{1,0:T(8,128)}) custom-call(s32[3]{0:T(128)} %pad_add_fusion.place_ref, s32[64,64]{1,0:T(8,128)} %segment_ref.3, s32[64,64]{1,0:T(8,128)} %tile_ref.3, s32[64]{0:T(128)} %order_ref.3, bf16[16,128,128]{2,1,0:T(8,128)(2,1)} %tiles_ref.3, bf16[4,16,128,128]{3,2,1,0:T(8,128)(2,1)} %paganin.1.refs_0_, ...), custom_call_target="tpu_custom_call" | custom-call | flops 536870912 | bytes 1048576 | tf_op jit(solution)/shard_map/backproject/pallas_call | solution.py:187
  36.6 1.3 %convert.12 = f16[4,4,128,128]{3,2,1,0:T(8,128)(2,1)S(1)} convert(f32[4,4,128,128]{3,2,1,0:T(8,128)} %get-tuple-element.8) | non-fusion elementwise | flops 262144 | bytes 1572864 | tf_op jit(solution)/shard_map/convert.2
  37.9 0.0 copy-start.1
  37.9 0.1 slice_bitcast_fusion.2
  38.0 2.3 %collective-permute-start.5 = (f16[4,128,128]{2,1,0:T(8,128)(2,1)S(1)}, f16[4,128,128]{2,1,0:T(8,128)(2,1)S(1)}, u32[]{:S(2)}, u32[]{:S(2)}) collective-permute-start(f16[4,128,128]{2,1,0:T(8,128)(2,1)S(1)} %get-tuple-element.15), channel_id=1, source_target_pairs={{0,6},{2,4},{4,2},{6,0},{8,14},{10,12},{12,10},{14,8},{1,7},{3,5},... | collective-permute-start | bytes 393224 | tf_op jit(solution)/shard_map/ppermute | solution.py:255
  40.4 4.7 %collective-permute-start.6 = (f16[4,128,128]{2,1,0:T(8,128)(2,1)S(1)}, f16[4,128,128]{2,1,0:T(8,128)(2,1)S(1)}, u32[]{:S(2)}, u32[]{:S(2)}) collective-permute-start(f16[4,128,128]{2,1,0:T(8,128)(2,1)S(1)} %get-tuple-element.17), channel_id=1, source_target_pairs={{0,4},{2,6},{4,0},{6,2},{8,12},{10,14},{12,8},{14,10},{1,5},{3,7},... | collective-permute-start | bytes 393224 | tf_op jit(solution)/shard_map/ppermute | solution.py:255
  45.1 1.5 %collective-permute-start.7 = (f16[4,128,128]{2,1,0:T(8,128)(2,1)S(1)}, f16[4,128,128]{2,1,0:T(8,128)(2,1)S(1)}, u32[]{:S(2)}, u32[]{:S(2)}) collective-permute-start(f16[4,128,128]{2,1,0:T(8,128)(2,1)S(1)} %get-tuple-element.16), channel_id=1, source_target_pairs={{0,2},{2,0},{4,6},{6,4},{8,10},{10,8},{12,14},{14,12},{1,3},{3,1},... | collective-permute-start | bytes 393224 | tf_op jit(solution)/shard_map/ppermute | solution.py:255
  46.6 3.0 %collective-permute-done.3 = f16[4,128,128]{2,1,0:T(8,128)(2,1)S(1)} collective-permute-done((f16[4,128,128]{2,1,0:T(8,128)(2,1)S(1)}, f16[4,128,128]{2,1,0:T(8,128)(2,1)S(1)}, u32[]{:S(2)}, u32[]{:S(2)}) %collective-permute-start.3) | collective-permute-done | bytes 131104 | tf_op jit(solution)/shard_map/ppermute | solution.py:250
  49.6 2.0 %collective-permute-done.4 = f16[4,128,128]{2,1,0:T(8,128)(2,1)S(1)} collective-permute-done((f16[4,128,128]{2,1,0:T(8,128)(2,1)S(1)}, f16[4,128,128]{2,1,0:T(8,128)(2,1)S(1)}, u32[]{:S(2)}, u32[]{:S(2)}) %collective-permute-start.4) | collective-permute-done | bytes 131104 | tf_op jit(solution)/shard_map/ppermute | solution.py:250
  51.7 1.2 %collective-permute-done.6 = f16[4,128,128]{2,1,0:T(8,128)(2,1)S(1)} collective-permute-done((f16[4,128,128]{2,1,0:T(8,128)(2,1)S(1)}, f16[4,128,128]{2,1,0:T(8,128)(2,1)S(1)}, u32[]{:S(2)}, u32[]{:S(2)}) %collective-permute-start.6) | collective-permute-done | bytes 131104 | tf_op jit(solution)/shard_map/ppermute | solution.py:255
  52.9 1.8 %fusion.6.rows_ref = f32[4,128,128]{2,1,0:T(8,128)} fusion(f16[4,128,128]{2,1,0:T(8,128)(2,1)S(1)} %collective-permute-done.7, f16[4,128,128]{2,1,0:T(8,128)(2,1)S(1)} %collective-permute-done.6, f16[4,128,128]{2,1,0:T(8,128)(2,1)S(1)} %collective-permute-done.5, f16[4,128,128]{2,1,0:T(8,128)(2,1)S(1)} %collective-permute-done.4, ...), kind=kLoop, calls=%fused_computation.10 | loop fusion | flops 917504 | bytes 1441792 | tf_op jit(solution)/shard_map/add | solution.py:258
  54.7 1.8 %regroup.1 = f32[8,4,32,128]{3,2,1,0:T(8,128)} custom-call(s32[8]{0:T(128)} %counts_ref.1, f32[4,128,128]{2,1,0:T(8,128)} %fusion.6.rows_ref), custom_call_target="tpu_custom_call" | custom-call | tf_op jit(solution)/shard_map/regroup/pallas_call | solution.py:219
  56.5 1.8 %multiply_convert_fusion = f16[8,4,32,128]{3,2,1,0:T(8,128)(2,1)} fusion(f32[8,4,32,128]{3,2,1,0:T(8,128)} %regroup.1), kind=kLoop, calls=%fused_computation.3 | loop fusion | flops 262144 | bytes 786432 | tf_op jit(solution)/shard_map/convert_element_type | solution.py:260
  58.3 4.0 %all-to-all-start = ((f16[8,4,32,128]{3,2,1,0:T(8,128)(2,1)}), f16[8,4,32,128]{3,2,1,0:T(8,128)(2,1)S(1)}, u32[]{:S(2)}, u32[]{:S(2)}) async-start(f16[8,4,32,128]{3,2,1,0:T(8,128)(2,1)} %multiply_convert_fusion), calls=%async_computation | async-start | bytes 524288 | tf_op jit(solution)/shard_map/all_to_all | solution.py:260
  62.3 0.6 dynamic_slice.3
  62.9 0.6 iota_compare_fusion
  63.5 1.2 %slice.7 = f32[1,1]{1,0:T(1,128)} slice(f32[8,128]{1,0:T(8,128)} %get-tuple-element.10), slice={[0:1], [0:1]} | slice | bytes 8 | tf_op jit(solution)/shard_map/slice | solution.py:262
  65.4 5.1 %all-to-all-done = f16[8,4,32,128]{3,2,1,0:T(8,128)(2,1)S(1)} async-done(((f16[8,4,32,128]{3,2,1,0:T(8,128)(2,1)}), f16[8,4,32,128]{3,2,1,0:T(8,128)(2,1)S(1)}, u32[]{:S(2)}, u32[]{:S(2)}) %all-to-all-start) | async-done | bytes 262176 | tf_op jit(solution)/shard_map/all_to_all | solution.py:260
  70.5 0.1 convert_multiply_fusion
  70.5 1.1 %fusion = f32[1,32,32,128]{3,2,1,0:T(8,128)} fusion(f32[32,32,128]{2,1,0:T(8,128)S(1)} %bitcast.37, pred[32]{0:T(512)(128)(4,1)S(1)} %iota_compare_fusion), kind=kLoop, calls=%fused_computation.1 | loop fusion | flops 131072 | bytes 1048608 | tf_op jit(solution)/shard_map/broadcast_in_dim | solution.py:265
  (6 shorter events, 0.0 us)
Async XLA Ops:
  11.1 4.5 %collective-permute-start = (bf16[4,16,128,128]{3,2,1,0:T(8,128)(2,1)}, bf16[4,16,128,128]{3,2,1,0:T(8,128)(2,1)S(1)}, u32[]{:S(2)}, u32[]{:S(2)}) collective-permute-start(bf16[4,16,128,128]{3,2,1,0:T(8,128)(2,1)} %paganin.1.refs_0_), channel_id=1, source_target_pairs={{0,1},{1,0},{2,3},{3,2},{4,5},{5,4},{6,7},{7,6},{8,9},{9,8},{10,11... | collective-permute-start | bytes 6291464 | tf_op jit(solution)/shard_map/ppermute | solution.py:242
  15.6 1.3 %copy-start = (bf16[4,16,128,128]{3,2,1,0:T(8,128)(2,1)}, bf16[4,16,128,128]{3,2,1,0:T(8,128)(2,1)S(1)}, u32[]{:S(2)}) copy-start(bf16[4,16,128,128]{3,2,1,0:T(8,128)(2,1)S(1)} %collective-permute-done.refs_1_) | copy-start | bytes 6291460
  23.0 17.4 %collective-permute-start.1 = (f16[4,128,128]{2,1,0:T(8,128)(2,1)S(1)}, f16[4,128,128]{2,1,0:T(8,128)(2,1)S(1)}, u32[]{:S(2)}, u32[]{:S(2)}) collective-permute-start(f16[4,128,128]{2,1,0:T(8,128)(2,1)S(1)} %get-tuple-element.11), channel_id=1, source_target_pairs={{0,14},{2,12},{4,10},{6,8},{8,6},{10,4},{12,2},{14,0},{1,15},{3,13... | collective-permute-start | bytes 393224 | tf_op jit(solution)/shard_map/ppermute | solution.py:250
  29.0 16.2 %collective-permute-start.2 = (f16[4,128,128]{2,1,0:T(8,128)(2,1)S(1)}, f16[4,128,128]{2,1,0:T(8,128)(2,1)S(1)}, u32[]{:S(2)}, u32[]{:S(2)}) collective-permute-start(f16[4,128,128]{2,1,0:T(8,128)(2,1)S(1)} %get-tuple-element.14), channel_id=1, source_target_pairs={{0,12},{2,14},{4,8},{6,10},{8,4},{10,6},{12,0},{14,2},{1,13},{3,15... | collective-permute-start | bytes 393224 | tf_op jit(solution)/shard_map/ppermute | solution.py:250
  29.2 20.4 %collective-permute-start.3 = (f16[4,128,128]{2,1,0:T(8,128)(2,1)S(1)}, f16[4,128,128]{2,1,0:T(8,128)(2,1)S(1)}, u32[]{:S(2)}, u32[]{:S(2)}) collective-permute-start(f16[4,128,128]{2,1,0:T(8,128)(2,1)S(1)} %get-tuple-element.13), channel_id=1, source_target_pairs={{0,10},{2,8},{4,14},{6,12},{8,2},{10,0},{12,6},{14,4},{1,11},{3,9}... | collective-permute-start | bytes 393224 | tf_op jit(solution)/shard_map/ppermute | solution.py:250
  29.9 21.7 %collective-permute-start.4 = (f16[4,128,128]{2,1,0:T(8,128)(2,1)S(1)}, f16[4,128,128]{2,1,0:T(8,128)(2,1)S(1)}, u32[]{:S(2)}, u32[]{:S(2)}) collective-permute-start(f16[4,128,128]{2,1,0:T(8,128)(2,1)S(1)} %get-tuple-element.12), channel_id=1, source_target_pairs={{0,8},{2,10},{4,12},{6,14},{8,0},{10,2},{12,4},{14,6},{1,9},{3,11}... | collective-permute-start | bytes 393224 | tf_op jit(solution)/shard_map/ppermute | solution.py:250
  37.9 24.3 %copy-start.1 = (s32[8]{0:T(128)S(1)}, s32[8]{0:T(128)}, u32[]{:S(2)}) copy-start(s32[8]{0:T(128)} %counts_ref.1) | copy-start | bytes 100
  38.0 13.6 %collective-permute-start.5 = (f16[4,128,128]{2,1,0:T(8,128)(2,1)S(1)}, f16[4,128,128]{2,1,0:T(8,128)(2,1)S(1)}, u32[]{:S(2)}, u32[]{:S(2)}) collective-permute-start(f16[4,128,128]{2,1,0:T(8,128)(2,1)S(1)} %get-tuple-element.15), channel_id=1, source_target_pairs={{0,6},{2,4},{4,2},{6,0},{8,14},{10,12},{12,10},{14,8},{1,7},{3,5},... | collective-permute-start | bytes 393224 | tf_op jit(solution)/shard_map/ppermute | solution.py:255
  40.4 12.5 %collective-permute-start.6 = (f16[4,128,128]{2,1,0:T(8,128)(2,1)S(1)}, f16[4,128,128]{2,1,0:T(8,128)(2,1)S(1)}, u32[]{:S(2)}, u32[]{:S(2)}) collective-permute-start(f16[4,128,128]{2,1,0:T(8,128)(2,1)S(1)} %get-tuple-element.17), channel_id=1, source_target_pairs={{0,4},{2,6},{4,0},{6,2},{8,12},{10,14},{12,8},{14,10},{1,5},{3,7},... | collective-permute-start | bytes 393224 | tf_op jit(solution)/shard_map/ppermute | solution.py:255
  45.1 7.8 %collective-permute-start.7 = (f16[4,128,128]{2,1,0:T(8,128)(2,1)S(1)}, f16[4,128,128]{2,1,0:T(8,128)(2,1)S(1)}, u32[]{:S(2)}, u32[]{:S(2)}) collective-permute-start(f16[4,128,128]{2,1,0:T(8,128)(2,1)S(1)} %get-tuple-element.16), channel_id=1, source_target_pairs={{0,2},{2,0},{4,6},{6,4},{8,10},{10,8},{12,14},{14,12},{1,3},{3,1},... | collective-permute-start | bytes 393224 | tf_op jit(solution)/shard_map/ppermute | solution.py:255
  58.3 12.2 %all-to-all-start = ((f16[8,4,32,128]{3,2,1,0:T(8,128)(2,1)}), f16[8,4,32,128]{3,2,1,0:T(8,128)(2,1)S(1)}, u32[]{:S(2)}, u32[]{:S(2)}) async-start(f16[8,4,32,128]{3,2,1,0:T(8,128)(2,1)} %multiply_convert_fusion), calls=%async_computation | async-start | bytes 524288 | tf_op jit(solution)/shard_map/all_to_all | solution.py:260

commit v3 on v2

--- a/solution.py
+++ b/solution.py
@@ -12,9 +12,10 @@
 paganin_alpha = 2.0
 lanes = 128
 sublanes = 8
-strands = 8
+strands = 16
 chunks = strands * sublanes
 pitch_pad = 8
+kernel_vmem = 24 << 20
 thickness_bound = 1.75
 send_bound = 60000.0
 
@@ -79,10 +80,10 @@
     def place(column):
         return column // span * pitch + column % span
 
-    for column in range(0, width, lanes):
-        turned = f_ref[0, :, column : column + lanes].T
-        modes_ref[pl.ds(place(column), lanes), :] = jnp.dot(
-            paired_parts(turned), forward_ref[...], preferred_element_type=jnp.float32
+    for column in range(0, width, span):
+        turned = [f_ref[0, :, start : start + lanes].T for start in range(column, column + span, lanes)]
+        modes_ref[pl.ds(place(column), span), :] = jnp.dot(
+            paired_parts(jnp.concatenate(turned, axis=0)), forward_ref[...], preferred_element_type=jnp.float32
         )
 
     root = powers_ref[pl.ds(0, sublanes), :]
@@ -104,15 +105,15 @@
         ends = sweep(zeros, order, False)
         sweep(carries(ends, powers_ref, direction), order, True)
 
-    for column in range(0, width, lanes):
+    for column in range(0, width, span):
         filtered = lax.dot_general(
             back_ref[...],
-            paired_parts(modes_ref[pl.ds(place(column), lanes), :]),
+            paired_parts(modes_ref[pl.ds(place(column), span), :]),
             (((1,), (1,)), ((), ())),
             preferred_element_type=jnp.float32,
         )
         thickness = (-jnp.log(filtered)).astype(jnp.bfloat16)
-        for part in range(lanes // edge):
+        for part in range(span // edge):
             out_ref[0, column // edge + part] = thickness[:, part * edge : (part + 1) * edge]
 
 
@@ -134,8 +135,9 @@
         out_specs=pl.BlockSpec((1, segments, row_total, voxel_edge), lambda a: (a, 0, 0, 0)),
         out_shape=jax.ShapeDtypeStruct((angle_count, segments, row_total, voxel_edge), jnp.bfloat16),
         scratch_shapes=[pltpu.VMEM((width + sublanes * pitch_pad, row_total), jnp.float32)],
+        compiler_params=pltpu.CompilerParams(vmem_limit_bytes=kernel_vmem),
         name="paganin",
-    )(forward, back, powers, intensity)
+    )(*[pltpu.with_memory_space_constraint(v, pltpu.HBM) for v in (forward, back, powers, intensity)])
 
 
 def send_scale(largest, angle_total, voxel_edge):
@@ -176,6 +178,10 @@
                 preferred_element_type=jnp.float32,
             )
             out_ref[chunk, block] = total * scale
+
+
+def resident(values):
+    return pltpu.with_memory_space_constraint(values, pltpu.VMEM)
 
 
 def backproject(partners, place, segment_ids, tile_ids, block_order, tiles, thickness, share):
@@ -197,8 +203,9 @@
             bytes_accessed=4 * blocks * row_total * edge,
             transcendentals=0,
         ),
+        compiler_params=pltpu.CompilerParams(vmem_limit_bytes=kernel_vmem),
         name="backproject",
-    )(place, segment_ids, tile_ids, block_order, tiles, *thickness)
+    )(place, segment_ids, tile_ids, block_order, tiles, *[resident(t) for t in thickness])
 
 
 def regroup_kernel(counts_ref, rows_ref, out_ref, padded_ref):
@@ -222,6 +229,7 @@
         out_specs=pl.BlockSpec(memory_space=pltpu.VMEM),
         out_shape=jax.ShapeDtypeStruct((group_total, share, capacity, edge), jnp.float32),
         scratch_shapes=[pltpu.VMEM((share, row_total + capacity, edge), jnp.float32)],
+        compiler_params=pltpu.CompilerParams(vmem_limit_bytes=kernel_vmem),
         name="regroup",
     )(counts, rows)
 

time: 72.2 us -> 62.7 us (0.87)
  other arithmetic: 8.67 us -> 3.06 us
  Pallas kernels: 22.1 us -> 16.9 us
  starting transfers between devices: 22 us -> 24.3 us
  local copies, waits for them, and re-layouts: 3.32 us -> 1.48 us
  waiting for transfers between devices: 14.8 us -> 15.9 us
    pallas_call x2, Pallas kernels: 9.27 us -> 6.3 us  [backproject(): pl.pallas_call(functools.partial(backproject_kernel, tuple(partners)), in...]
    another operation x2, other arithmetic: 2.65 us -> 0.2 us
    ppermute x7, starting transfers between devices: 17.6 us -> 19.7 us  [per_device(): parts.append(lax.ppermute(partial.astype(jnp.float16), 'angle', swap))]
    add x1, other arithmetic: 1.79 us -> 0.14 us  [per_device(): rows = rows + part.astype(jnp.float32)]
    unnamed x4 -> x10, local copies, waits for them, and re-layouts: 1.32 us -> 0.02 us
    pallas_call x1, Pallas kernels: 1.81 us -> 0.6 us  [regroup(): pl.pallas_call(regroup_kernel, in_specs=[pl.BlockSpec(memory_space=pltpu....]
    pallas_call x1, Pallas kernels: 11.1 us -> 10 us  [paganin_thickness(): pl.pallas_call(filter_kernel, grid=(angle_count,), in_specs=[pl.BlockSpec...]
    convert_element_type x1, other arithmetic: 1.8 us -> 0.77 us  [per_device(): slots.astype(jnp.float16)]
  transfers between devices with their start and end apart: 9 -> 9, of which waited for: 5 -> 5; matrix products, arithmetic and copies ran while one was open for 6% -> 4% of each run, Pallas kernels for 6% -> 5%
where the time goes in v3:
time: 62.7 us; the launch traced here: 62.4 us
  starting transfers between devices  24.3 us (39%)
  Pallas kernels  16.9 us (27%)
  waiting for transfers between devices  15.9 us (25%)
  other arithmetic  3.06 us (5%)
  local copies, waits for them, and re-layouts  1.48 us (2%)
  between operations  0.79 us (1%)
    ppermute x7, starting transfers between devices, per_device(): parts.append(lax.ppermute(partial.astype(jnp.float16), 'angle', swap))  19.7 us
    pallas_call x1, Pallas kernels, paganin_thickness(): pl.pallas_call(filter_kernel, grid=(angle_count,), in_specs=[pl.BlockSpec...  10 us
    ppermute x7, waiting for transfers between devices, per_device(): parts.append(lax.ppermute(partial.astype(jnp.float16), 'angle', swap))  6.47 us
    pallas_call x2, Pallas kernels, backproject(): pl.pallas_call(functools.partial(backproject_kernel, tuple(partners)), in...  6.3 us
    all_to_all x1, waiting for transfers between devices, per_device(): lax.all_to_all(slots.astype(jnp.float16), 'angle', split_axis=0, concat_a...  5.58 us
    all_to_all x1, starting transfers between devices, per_device(): lax.all_to_all(slots.astype(jnp.float16), 'angle', split_axis=0, concat_a...  3.95 us
    ppermute x1, waiting for transfers between devices, per_device(): sources.append(lax.ppermute(thickness, 'tile', ring))  3.84 us
  transfers between devices with their start and end apart: 9, of which 5 were waited for; matrix products, arithmetic and copies ran while one was open for 4% of the time, Pallas kernels for 5%

profile of v3, /device:TPU:0, one launch (start us, length us, event | category | flops | bytes accessed | tf_op | source)
XLA Modules:
  0.0 62.4 jit_solution(4415054810932791074)
XLA Ops:
  0.0 10.0 %paganin.1.refs_0_ = bf16[4,16,128,128]{3,2,1,0:T(8,128)(2,1)S(1)} custom-call(bf16[384,128]{1,0:T(8,128)(2,1)} %constant.27.clone.forward_ref, bf16[128,384]{1,0:T(8,128)(2,1)} %constant.28.clone.back_ref, f32[72,128]{1,0:T(8,128)} %constant.29.clone.powers_ref, f32[4,128,2048]{2,1,0:T(8,128)} %f_ref.1), custom_call_target="tpu_custom_call" | custom-call | tf_op jit(solution)/shard_map/paganin/pallas_call | solution.py:126
  10.0 0.6 collective-permute-start
  10.6 0.1 pad_add_fusion.place_ref
  10.7 3.8 %collective-permute-done.refs_1_ = bf16[4,16,128,128]{3,2,1,0:T(8,128)(2,1)} collective-permute-done((bf16[4,16,128,128]{3,2,1,0:T(8,128)(2,1)S(1)}, bf16[4,16,128,128]{3,2,1,0:T(8,128)(2,1)}, u32[]{:S(2)}, u32[]{:S(2)}) %collective-permute-start) | collective-permute-done | bytes 2097184 | tf_op jit(solution)/shard_map/ppermute | solution.py:250
  14.5 2.9 %backproject.3 = (f32[4,4,128,128]{3,2,1,0:T(8,128)S(1)}, f32[8,128]{1,0:T(8,128)S(1)}) custom-call(s32[3]{0:T(128)S(1)} %pad_add_fusion.place_ref, s32[64,64]{1,0:T(8,128)S(1)} %copy-done.1, s32[64,64]{1,0:T(8,128)S(1)} %copy-done.2, s32[64]{0:T(128)S(1)} %copy-done.3, bf16[16,128,128]{2,1,0:T(8,128)(2,1)S(1)} %copy-done, ...), custom_call_target="tpu_custom_call" | custom-call | flops 536870912 | bytes 1048576 | tf_op jit(solution)/shard_map/backproject/pallas_call | solution.py:193
  17.5 0.1 convert.11
  17.6 0.1 slice_bitcast_fusion.6
  17.7 6.0 %collective-permute-start.1 = (f16[4,128,128]{2,1,0:T(8,128)(2,1)S(1)}, f16[4,128,128]{2,1,0:T(8,128)(2,1)S(1)}, u32[]{:S(2)}, u32[]{:S(2)}) collective-permute-start(f16[4,128,128]{2,1,0:T(8,128)(2,1)S(1)} %get-tuple-element.11), channel_id=1, source_target_pairs={{0,14},{2,12},{4,10},{6,8},{8,6},{10,4},{12,2},{14,0},{1,15},{3,13... | collective-permute-start | bytes 393224 | tf_op jit(solution)/shard_map/ppermute | solution.py:258
  23.7 0.1 collective-permute-start.2
  23.9 0.8 %collective-permute-start.3 = (f16[4,128,128]{2,1,0:T(8,128)(2,1)S(1)}, f16[4,128,128]{2,1,0:T(8,128)(2,1)S(1)}, u32[]{:S(2)}, u32[]{:S(2)}) collective-permute-start(f16[4,128,128]{2,1,0:T(8,128)(2,1)S(1)} %get-tuple-element.13), channel_id=1, source_target_pairs={{0,10},{2,8},{4,14},{6,12},{8,2},{10,0},{12,6},{14,4},{1,11},{3,9}... | collective-permute-start | bytes 393224 | tf_op jit(solution)/shard_map/ppermute | solution.py:258
  24.7 2.0 %collective-permute-start.4 = (f16[4,128,128]{2,1,0:T(8,128)(2,1)S(1)}, f16[4,128,128]{2,1,0:T(8,128)(2,1)S(1)}, u32[]{:S(2)}, u32[]{:S(2)}) collective-permute-start(f16[4,128,128]{2,1,0:T(8,128)(2,1)S(1)} %get-tuple-element.12), channel_id=1, source_target_pairs={{0,8},{2,10},{4,12},{6,14},{8,0},{10,2},{12,4},{14,6},{1,9},{3,11}... | collective-permute-start | bytes 393224 | tf_op jit(solution)/shard_map/ppermute | solution.py:258
  26.7 3.4 %backproject.2 = (f32[4,4,128,128]{3,2,1,0:T(8,128)S(1)}, f32[8,128]{1,0:T(8,128)}) custom-call(s32[3]{0:T(128)S(1)} %pad_add_fusion.place_ref, s32[64,64]{1,0:T(8,128)S(1)} %copy-done.1, s32[64,64]{1,0:T(8,128)S(1)} %copy-done.2, s32[64]{0:T(128)S(1)} %copy-done.3, bf16[16,128,128]{2,1,0:T(8,128)(2,1)S(1)} %copy-done, ...), custom_call_target="tpu_custom_call" | custom-call | flops 536870912 | bytes 1048576 | tf_op jit(solution)/shard_map/backproject/pallas_call | solution.py:193
  30.1 0.1 convert.12
  30.3 0.1 slice_bitcast_fusion.2
  30.3 2.4 %collective-permute-start.5 = (f16[4,128,128]{2,1,0:T(8,128)(2,1)S(1)}, f16[4,128,128]{2,1,0:T(8,128)(2,1)S(1)}, u32[]{:S(2)}, u32[]{:S(2)}) collective-permute-start(f16[4,128,128]{2,1,0:T(8,128)(2,1)S(1)} %get-tuple-element.15), channel_id=1, source_target_pairs={{0,6},{2,4},{4,2},{6,0},{8,14},{10,12},{12,10},{14,8},{1,7},{3,5},... | collective-permute-start | bytes 393224 | tf_op jit(solution)/shard_map/ppermute | solution.py:263
  32.7 0.0 collective-permute-done.1
  32.7 6.9 %collective-permute-start.6 = (f16[4,128,128]{2,1,0:T(8,128)(2,1)S(1)}, f16[4,128,128]{2,1,0:T(8,128)(2,1)S(1)}, u32[]{:S(2)}, u32[]{:S(2)}) collective-permute-start(f16[4,128,128]{2,1,0:T(8,128)(2,1)S(1)} %get-tuple-element.17), channel_id=1, source_target_pairs={{0,4},{2,6},{4,0},{6,2},{8,12},{10,14},{12,8},{14,10},{1,5},{3,7},... | collective-permute-start | bytes 393224 | tf_op jit(solution)/shard_map/ppermute | solution.py:263
  39.6 1.5 %collective-permute-start.7 = (f16[4,128,128]{2,1,0:T(8,128)(2,1)S(1)}, f16[4,128,128]{2,1,0:T(8,128)(2,1)S(1)}, u32[]{:S(2)}, u32[]{:S(2)}) collective-permute-start(f16[4,128,128]{2,1,0:T(8,128)(2,1)S(1)} %get-tuple-element.16), channel_id=1, source_target_pairs={{0,2},{2,0},{4,6},{6,4},{8,10},{10,8},{12,14},{14,12},{1,3},{3,1},... | collective-permute-start | bytes 393224 | tf_op jit(solution)/shard_map/ppermute | solution.py:263
  41.0 3.3 %collective-permute-done.3 = f16[4,128,128]{2,1,0:T(8,128)(2,1)S(1)} collective-permute-done((f16[4,128,128]{2,1,0:T(8,128)(2,1)S(1)}, f16[4,128,128]{2,1,0:T(8,128)(2,1)S(1)}, u32[]{:S(2)}, u32[]{:S(2)}) %collective-permute-start.3) | collective-permute-done | bytes 131104 | tf_op jit(solution)/shard_map/ppermute | solution.py:258
  44.4 2.0 %collective-permute-done.4 = f16[4,128,128]{2,1,0:T(8,128)(2,1)S(1)} collective-permute-done((f16[4,128,128]{2,1,0:T(8,128)(2,1)S(1)}, f16[4,128,128]{2,1,0:T(8,128)(2,1)S(1)}, u32[]{:S(2)}, u32[]{:S(2)}) %collective-permute-start.4) | collective-permute-done | bytes 131104 | tf_op jit(solution)/shard_map/ppermute | solution.py:258
  46.4 0.0 collective-permute-done.5
  46.4 1.1 %collective-permute-done.6 = f16[4,128,128]{2,1,0:T(8,128)(2,1)S(1)} collective-permute-done((f16[4,128,128]{2,1,0:T(8,128)(2,1)S(1)}, f16[4,128,128]{2,1,0:T(8,128)(2,1)S(1)}, u32[]{:S(2)}, u32[]{:S(2)}) %collective-permute-start.6) | collective-permute-done | bytes 131104 | tf_op jit(solution)/shard_map/ppermute | solution.py:263
  47.5 0.1 fusion.6.rows_ref
  47.6 0.6 regroup.1
  48.3 0.8 %multiply_convert_fusion = f16[8,4,32,128]{3,2,1,0:T(8,128)(2,1)} fusion(f32[8,4,32,128]{3,2,1,0:T(8,128)S(1)} %regroup.1), kind=kLoop, calls=%fused_computation.3 | loop fusion | flops 262144 | bytes 786432 | tf_op jit(solution)/shard_map/convert_element_type | solution.py:268
  49.0 4.0 %all-to-all-start = ((f16[8,4,32,128]{3,2,1,0:T(8,128)(2,1)}), f16[8,4,32,128]{3,2,1,0:T(8,128)(2,1)S(1)}, u32[]{:S(2)}, u32[]{:S(2)}) async-start(f16[8,4,32,128]{3,2,1,0:T(8,128)(2,1)} %multiply_convert_fusion), calls=%async_computation | async-start | bytes 524288 | tf_op jit(solution)/shard_map/all_to_all | solution.py:268
  53.0 0.7 %dynamic_slice.3 = s32[1]{0:T(128)} dynamic-slice(s32[8]{0:T(128)S(1)} %copy-done.4, s32[]{:T(128)S(6)} %select_n.7), dynamic_slice_sizes={1} | dynamic-slice | bytes 12 | tf_op jit(solution)/shard_map/dynamic_slice | solution.py:271
  53.6 0.7 %iota_compare_fusion = pred[32]{0:T(512)(128)(4,1)S(1)} fusion(s32[]{:T(128)} %bitcast), kind=kLoop, calls=%fused_computation.19 | loop fusion | flops 32 | bytes 36 | tf_op jit(solution)/shard_map/lt | solution.py:271
  54.3 0.6 slice.7
  55.6 5.6 %all-to-all-done = f16[8,4,32,128]{3,2,1,0:T(8,128)(2,1)S(1)} async-done(((f16[8,4,32,128]{3,2,1,0:T(8,128)(2,1)}), f16[8,4,32,128]{3,2,1,0:T(8,128)(2,1)S(1)}, u32[]{:S(2)}, u32[]{:S(2)}) %all-to-all-start) | async-done | bytes 262176 | tf_op jit(solution)/shard_map/all_to_all | solution.py:268
  61.2 0.1 convert_multiply_fusion
  61.3 1.1 %fusion = f32[1,32,32,128]{3,2,1,0:T(8,128)} fusion(f32[32,32,128]{2,1,0:T(8,128)S(1)} %bitcast.37, pred[32]{0:T(512)(128)(4,1)S(1)} %iota_compare_fusion), kind=kLoop, calls=%fused_computation.1 | loop fusion | flops 131072 | bytes 1048608 | tf_op jit(solution)/shard_map/broadcast_in_dim | solution.py:273
  (12 shorter events, 0.0 us)
Async XLA Ops:
  0.0 14.5 %copy-start.1 = (s32[64,64]{1,0:T(8,128)S(1)}, s32[64,64]{1,0:T(8,128)}, u32[]{:S(2)}) copy-start(s32[64,64]{1,0:T(8,128)} %segment_ref.3) | copy-start | bytes 49156
  0.0 14.5 %copy-start.2 = (s32[64,64]{1,0:T(8,128)S(1)}, s32[64,64]{1,0:T(8,128)}, u32[]{:S(2)}) copy-start(s32[64,64]{1,0:T(8,128)} %tile_ref.3) | copy-start | bytes 49156
  0.0 14.5 %copy-start.3 = (s32[64]{0:T(128)S(1)}, s32[64]{0:T(128)}, u32[]{:S(2)}) copy-start(s32[64]{0:T(128)} %order_ref.3) | copy-start | bytes 772
  0.0 14.5 %copy-start = (bf16[16,128,128]{2,1,0:T(8,128)(2,1)S(1)}, bf16[16,128,128]{2,1,0:T(8,128)(2,1)}, u32[]{:S(2)}) copy-start(bf16[16,128,128]{2,1,0:T(8,128)(2,1)} %tiles_ref.3) | copy-start | bytes 1572868
  10.0 4.5 %collective-permute-start = (bf16[4,16,128,128]{3,2,1,0:T(8,128)(2,1)S(1)}, bf16[4,16,128,128]{3,2,1,0:T(8,128)(2,1)}, u32[]{:S(2)}, u32[]{:S(2)}) collective-permute-start(bf16[4,16,128,128]{3,2,1,0:T(8,128)(2,1)S(1)} %paganin.1.refs_0_), channel_id=1, source_target_pairs={{0,1},{1,0},{2,3},{3,2},{4,5},{5,4},{6,7},{7,6},{8,9},{9,8},{10,11... | collective-permute-start | bytes 6291464 | tf_op jit(solution)/shard_map/ppermute | solution.py:250
  17.7 15.0 %collective-permute-start.1 = (f16[4,128,128]{2,1,0:T(8,128)(2,1)S(1)}, f16[4,128,128]{2,1,0:T(8,128)(2,1)S(1)}, u32[]{:S(2)}, u32[]{:S(2)}) collective-permute-start(f16[4,128,128]{2,1,0:T(8,128)(2,1)S(1)} %get-tuple-element.11), channel_id=1, source_target_pairs={{0,14},{2,12},{4,10},{6,8},{8,6},{10,4},{12,2},{14,0},{1,15},{3,13... | collective-permute-start | bytes 393224 | tf_op jit(solution)/shard_map/ppermute | solution.py:258
  23.7 15.8 %collective-permute-start.2 = (f16[4,128,128]{2,1,0:T(8,128)(2,1)S(1)}, f16[4,128,128]{2,1,0:T(8,128)(2,1)S(1)}, u32[]{:S(2)}, u32[]{:S(2)}) collective-permute-start(f16[4,128,128]{2,1,0:T(8,128)(2,1)S(1)} %get-tuple-element.14), channel_id=1, source_target_pairs={{0,12},{2,14},{4,8},{6,10},{8,4},{10,6},{12,0},{14,2},{1,13},{3,15... | collective-permute-start | bytes 393224 | tf_op jit(solution)/shard_map/ppermute | solution.py:258
  23.9 20.5 %collective-permute-start.3 = (f16[4,128,128]{2,1,0:T(8,128)(2,1)S(1)}, f16[4,128,128]{2,1,0:T(8,128)(2,1)S(1)}, u32[]{:S(2)}, u32[]{:S(2)}) collective-permute-start(f16[4,128,128]{2,1,0:T(8,128)(2,1)S(1)} %get-tuple-element.13), channel_id=1, source_target_pairs={{0,10},{2,8},{4,14},{6,12},{8,2},{10,0},{12,6},{14,4},{1,11},{3,9}... | collective-permute-start | bytes 393224 | tf_op jit(solution)/shard_map/ppermute | solution.py:258
  24.7 21.7 %collective-permute-start.4 = (f16[4,128,128]{2,1,0:T(8,128)(2,1)S(1)}, f16[4,128,128]{2,1,0:T(8,128)(2,1)S(1)}, u32[]{:S(2)}, u32[]{:S(2)}) collective-permute-start(f16[4,128,128]{2,1,0:T(8,128)(2,1)S(1)} %get-tuple-element.12), channel_id=1, source_target_pairs={{0,8},{2,10},{4,12},{6,14},{8,0},{10,2},{12,4},{14,6},{1,9},{3,11}... | collective-permute-start | bytes 393224 | tf_op jit(solution)/shard_map/ppermute | solution.py:258
  30.1 17.5 %copy-start.4 = (s32[8]{0:T(128)S(1)}, s32[8]{0:T(128)}, u32[]{:S(2)}) copy-start(s32[8]{0:T(128)} %counts_ref.1) | copy-start | bytes 100
  30.3 16.0 %collective-permute-start.5 = (f16[4,128,128]{2,1,0:T(8,128)(2,1)S(1)}, f16[4,128,128]{2,1,0:T(8,128)(2,1)S(1)}, u32[]{:S(2)}, u32[]{:S(2)}) collective-permute-start(f16[4,128,128]{2,1,0:T(8,128)(2,1)S(1)} %get-tuple-element.15), channel_id=1, source_target_pairs={{0,6},{2,4},{4,2},{6,0},{8,14},{10,12},{12,10},{14,8},{1,7},{3,5},... | collective-permute-start | bytes 393224 | tf_op jit(solution)/shard_map/ppermute | solution.py:263
  32.7 14.8 %collective-permute-start.6 = (f16[4,128,128]{2,1,0:T(8,128)(2,1)S(1)}, f16[4,128,128]{2,1,0:T(8,128)(2,1)S(1)}, u32[]{:S(2)}, u32[]{:S(2)}) collective-permute-start(f16[4,128,128]{2,1,0:T(8,128)(2,1)S(1)} %get-tuple-element.17), channel_id=1, source_target_pairs={{0,4},{2,6},{4,0},{6,2},{8,12},{10,14},{12,8},{14,10},{1,5},{3,7},... | collective-permute-start | bytes 393224 | tf_op jit(solution)/shard_map/ppermute | solution.py:263
  39.6 7.9 %collective-permute-start.7 = (f16[4,128,128]{2,1,0:T(8,128)(2,1)S(1)}, f16[4,128,128]{2,1,0:T(8,128)(2,1)S(1)}, u32[]{:S(2)}, u32[]{:S(2)}) collective-permute-start(f16[4,128,128]{2,1,0:T(8,128)(2,1)S(1)} %get-tuple-element.16), channel_id=1, source_target_pairs={{0,2},{2,0},{4,6},{6,4},{8,10},{10,8},{12,14},{14,12},{1,3},{3,1},... | collective-permute-start | bytes 393224 | tf_op jit(solution)/shard_map/ppermute | solution.py:263
  49.0 12.2 %all-to-all-start = ((f16[8,4,32,128]{3,2,1,0:T(8,128)(2,1)}), f16[8,4,32,128]{3,2,1,0:T(8,128)(2,1)S(1)}, u32[]{:S(2)}, u32[]{:S(2)}) async-start(f16[8,4,32,128]{3,2,1,0:T(8,128)(2,1)} %multiply_convert_fusion), calls=%async_computation | async-start | bytes 524288 | tf_op jit(solution)/shard_map/all_to_all | solution.py:268

commit v4 on v3

--- a/solution.py
+++ b/solution.py
@@ -242,7 +242,11 @@
     group = lax.axis_index("angle")
     capacity = 2 * row_total // group_total
     share = block_order.shape[0] // (tile_total * group_total)
-    assert group_total & (group_total - 1) == 0
+    assert group_total >= 4 and group_total & (group_total - 1) == 0
+
+    def swap(values, partner):
+        return lax.ppermute(values, "angle", [(i, i ^ partner) for i in range(group_total)])
+
     thickness = paganin_thickness(intensity, voxel_edge)
     sources = [thickness]
     for shift in range(1, tile_total):
@@ -250,18 +254,20 @@
         sources.append(lax.ppermute(thickness, "tile", ring))
     place = jnp.stack([group, lax.axis_index("tile"), jnp.int32(group_total)]).astype(jnp.int32)
     tables = (place, segment_ids, tile_ids, block_order, tiles, sources, share)
-    half = max(1, group_total // 2)
-    far, unscale = backproject(range(half, group_total)[::-1], *tables)
-    parts = []
-    for partner, partial in zip(range(half, group_total)[::-1], far):
-        swap = [(i, i ^ partner) for i in range(group_total)]
-        parts.append(lax.ppermute(partial.astype(jnp.float16), "angle", swap))
-    near, _ = backproject(range(half)[::-1], *tables)
-    for partner, partial in zip(range(half)[::-1], near):
-        swap = [(i, i ^ partner) for i in range(group_total)]
-        if partner:
-            parts.append(lax.ppermute(partial.astype(jnp.float16), "angle", swap))
-    rows = near[half - 1]
+    half = group_total // 2
+    far = list(range(half, group_total, 2))
+    near = list(range(0, half, 2))
+    far_odd, unscale = backproject([k + 1 for k in far], *tables)
+    near_odd, _ = backproject([k + 1 for k in near], *tables)
+    even, _ = backproject(far + near, *tables)
+    far_sums = even[: len(far)] + swap(far_odd.astype(jnp.float16), 1).astype(jnp.float32)
+    sent = far_sums.astype(jnp.float16)
+    parts = [swap(sent[i], k) for i, k in enumerate(far)]
+    near_odd = near_odd.astype(jnp.float16)
+    near_odd, _ = lax.optimization_barrier((near_odd, sent))
+    near_sums = even[len(far) :] + swap(near_odd, 1).astype(jnp.float32)
+    parts += [swap(near_sums[i].astype(jnp.float16), k) for i, k in enumerate(near) if k]
+    rows = near_sums[0]
     for part in parts:
         rows = rows + part.astype(jnp.float32)
     slots = regroup(counts, rows, group_total, capacity) * (1.0 / group_total)

time: 62.7 us -> 58.1 us (0.927)
  starting transfers between devices: 24.3 us -> 15.2 us
  waiting for transfers between devices: 15.9 us -> 18.4 us
  Pallas kernels: 16.9 us -> 19.2 us
    ppermute x7 -> x5, starting transfers between devices: 19.7 us -> 10.1 us  [swap(): lax.ppermute(values, 'angle', [(i, i ^ partner) for i in range(group_tota...]
    pallas_call x2 -> x3, Pallas kernels: 6.3 us -> 8.6 us  [backproject(): pl.pallas_call(functools.partial(backproject_kernel, tuple(partners)), in...]
    ppermute x7 -> x5, waiting for transfers between devices: 6.47 us -> 8.74 us  [swap(): lax.ppermute(values, 'angle', [(i, i ^ partner) for i in range(group_tota...]
  transfers between devices with their start and end apart: 9 -> 7, of which waited for: 5 -> 6; matrix products, arithmetic and copies ran while one was open for 4% -> 4% of each run, Pallas kernels for 5% -> 11%
where the time goes in v4:
time: 58.1 us; the launch traced here: 57.7 us
  Pallas kernels  19.2 us (33%)
  waiting for transfers between devices  18.4 us (32%)
  starting transfers between devices  15.2 us (26%)
  other arithmetic  2.99 us (5%)
  local copies, waits for them, and re-layouts  1.21 us (2%)
  between operations  0.74 us (1%)
    ppermute x5, starting transfers between devices, swap(): lax.ppermute(values, 'angle', [(i, i ^ partner) for i in range(group_tota...  10.1 us
    pallas_call x1, Pallas kernels, paganin_thickness(): pl.pallas_call(filter_kernel, grid=(angle_count,), in_specs=[pl.BlockSpec...  10 us
    ppermute x5, waiting for transfers between devices, swap(): lax.ppermute(values, 'angle', [(i, i ^ partner) for i in range(group_tota...  8.74 us
    pallas_call x3, Pallas kernels, backproject(): pl.pallas_call(functools.partial(backproject_kernel, tuple(partners)), in...  8.6 us
    all_to_all x1, waiting for transfers between devices, per_device(): lax.all_to_all(slots.astype(jnp.float16), 'angle', split_axis=0, concat_a...  5.8 us
    all_to_all x1, starting transfers between devices, per_device(): lax.all_to_all(slots.astype(jnp.float16), 'angle', split_axis=0, concat_a...  4.52 us
    ppermute x1, waiting for transfers between devices, per_device(): sources.append(lax.ppermute(thickness, 'tile', ring))  3.84 us
  transfers between devices with their start and end apart: 7, of which 6 were waited for; matrix products, arithmetic and copies ran while one was open for 4% of the time, Pallas kernels for 11%

profile of v4, /device:TPU:0, one launch (start us, length us, event | category | flops | bytes accessed | tf_op | source)
XLA Modules:
  0.0 57.7 jit_solution(17813006333271544544)
XLA Ops:
  0.0 10.0 %paganin.1.refs_0_ = bf16[4,16,128,128]{3,2,1,0:T(8,128)(2,1)S(1)} custom-call(bf16[384,128]{1,0:T(8,128)(2,1)} %constant.27.clone.forward_ref, bf16[128,384]{1,0:T(8,128)(2,1)} %constant.28.clone.back_ref, f32[72,128]{1,0:T(8,128)} %constant.29.clone.powers_ref, f32[4,128,2048]{2,1,0:T(8,128)} %f_ref.1), custom_call_target="tpu_custom_call" | custom-call | tf_op jit(solution)/shard_map/paganin/pallas_call | solution.py:126
  10.0 0.6 %collective-permute-start = (bf16[4,16,128,128]{3,2,1,0:T(8,128)(2,1)S(1)}, bf16[4,16,128,128]{3,2,1,0:T(8,128)(2,1)}, u32[]{:S(2)}, u32[]{:S(2)}) collective-permute-start(bf16[4,16,128,128]{3,2,1,0:T(8,128)(2,1)S(1)} %paganin.1.refs_0_), channel_id=1, source_target_pairs={{0,1},{1,0},{2,3},{3,2},{4,5},{5,4},{6,7},{7,6},{8,9},{9,8},{10,11... | collective-permute-start | bytes 6291464 | tf_op jit(solution)/shard_map/ppermute | solution.py:254
  10.6 0.1 pad_add_fusion.place_ref
  10.7 3.8 %collective-permute-done.refs_1_ = bf16[4,16,128,128]{3,2,1,0:T(8,128)(2,1)} collective-permute-done((bf16[4,16,128,128]{3,2,1,0:T(8,128)(2,1)S(1)}, bf16[4,16,128,128]{3,2,1,0:T(8,128)(2,1)}, u32[]{:S(2)}, u32[]{:S(2)}) %collective-permute-start) | collective-permute-done | bytes 2097184 | tf_op jit(solution)/shard_map/ppermute | solution.py:254
  14.5 0.0 copy-done.1
  14.5 0.0 copy-done.2
  14.5 2.4 %backproject.5 = (f32[2,4,128,128]{3,2,1,0:T(8,128)S(1)}, f32[8,128]{1,0:T(8,128)S(1)}) custom-call(s32[3]{0:T(128)S(1)} %pad_add_fusion.place_ref, s32[64,64]{1,0:T(8,128)S(1)} %copy-done.1, s32[64,64]{1,0:T(8,128)S(1)} %copy-done.2, s32[64]{0:T(128)S(1)} %copy-done.3, bf16[16,128,128]{2,1,0:T(8,128)(2,1)S(1)} %copy-done, ...), custom_call_target="tpu_custom_call" | custom-call | flops 268435456 | bytes 524288 | tf_op jit(solution)/shard_map/backproject/pallas_call | solution.py:193
  17.0 2.9 %collective-permute-start.1 = (f16[2,4,128,128]{3,2,1,0:T(8,128)(2,1)S(1)}, f16[2,4,128,128]{3,2,1,0:T(8,128)(2,1)S(1)}, u32[]{:S(2)}, u32[]{:S(2)}) collective-permute-start(f16[2,4,128,128]{3,2,1,0:T(8,128)(2,1)S(1)} %convert_element_type.36), channel_id=1, source_target_pairs={{0,2},{2,0},{4,6},{6,4},{8,10},{10,8},{12,14},{14,12},{1,3},{3,1},... | collective-permute-start | bytes 786440 | tf_op jit(solution)/shard_map/ppermute | solution.py:248
  19.9 2.8 %backproject.4 = (f32[2,4,128,128]{3,2,1,0:T(8,128)S(1)}, f32[8,128]{1,0:T(8,128)}) custom-call(s32[3]{0:T(128)S(1)} %pad_add_fusion.place_ref, s32[64,64]{1,0:T(8,128)S(1)} %copy-done.1, s32[64,64]{1,0:T(8,128)S(1)} %copy-done.2, s32[64]{0:T(128)S(1)} %copy-done.3, bf16[16,128,128]{2,1,0:T(8,128)(2,1)S(1)} %copy-done, ...), custom_call_target="tpu_custom_call" | custom-call | flops 268435456 | bytes 524288 | tf_op jit(solution)/shard_map/backproject/pallas_call | solution.py:193
  22.8 3.4 %backproject.3 = (f32[4,4,128,128]{3,2,1,0:T(8,128)S(1)}, f32[8,128]{1,0:T(8,128)}) custom-call(s32[3]{0:T(128)S(1)} %pad_add_fusion.place_ref, s32[64,64]{1,0:T(8,128)S(1)} %copy-done.1, s32[64,64]{1,0:T(8,128)S(1)} %copy-done.2, s32[64]{0:T(128)S(1)} %copy-done.3, bf16[16,128,128]{2,1,0:T(8,128)(2,1)S(1)} %copy-done, ...), custom_call_target="tpu_custom_call" | custom-call | flops 536870912 | bytes 1048576 | tf_op jit(solution)/shard_map/backproject/pallas_call | solution.py:193
  26.2 0.3 collective-permute-done.1
  26.5 0.1 add_convert_fusion
  26.6 1.8 %collective-permute-start.2 = (f16[2,4,128,128]{3,2,1,0:T(8,128)(2,1)S(1)}, f16[2,4,128,128]{3,2,1,0:T(8,128)(2,1)S(1)}, u32[]{:S(2)}, u32[]{:S(2)}) collective-permute-start(f16[2,4,128,128]{3,2,1,0:T(8,128)(2,1)S(1)} %convert_element_type.35), channel_id=1, source_target_pairs={{0,2},{2,0},{4,6},{6,4},{8,10},{10,8},{12,14},{14,12},{1,3},{3,1},... | collective-permute-start | bytes 786440 | tf_op jit(solution)/shard_map/ppermute | solution.py:248
  28.4 0.1 slice_bitcast_fusion.2
  28.4 3.7 %collective-permute-start.4 = (f16[4,128,128]{2,1,0:T(8,128)(2,1)S(1)}, f16[4,128,128]{2,1,0:T(8,128)(2,1)S(1)}, u32[]{:S(2)}, u32[]{:S(2)}) collective-permute-start(f16[4,128,128]{2,1,0:T(8,128)(2,1)S(1)} %get-tuple-element.16), channel_id=1, source_target_pairs={{0,12},{2,14},{4,8},{6,10},{8,4},{10,6},{12,0},{14,2},{1,13},{3,15... | collective-permute-start | bytes 393224 | tf_op jit(solution)/shard_map/ppermute | solution.py:248
  32.2 0.0 collective-permute-start.3
  32.2 2.2 %collective-permute-done.2 = f16[2,4,128,128]{3,2,1,0:T(8,128)(2,1)S(1)} collective-permute-done((f16[2,4,128,128]{3,2,1,0:T(8,128)(2,1)S(1)}, f16[2,4,128,128]{3,2,1,0:T(8,128)(2,1)S(1)}, u32[]{:S(2)}, u32[]{:S(2)}) %collective-permute-start.2) | collective-permute-done | bytes 262176 | tf_op jit(solution)/shard_map/ppermute | solution.py:248
  34.4 0.1 convert_add_fusion
  34.5 1.6 %collective-permute-start.5 = (f16[4,128,128]{2,1,0:T(8,128)(2,1)S(1)}, f16[4,128,128]{2,1,0:T(8,128)(2,1)S(1)}, u32[]{:S(2)}, u32[]{:S(2)}) collective-permute-start(f16[4,128,128]{2,1,0:T(8,128)(2,1)S(1)} %fusion.4), channel_id=1, source_target_pairs={{0,4},{2,6},{4,0},{6,2},{8,12},{10,14},{12,8},{14,10},{1,5},{3,7},... | collective-permute-start | bytes 393224 | tf_op jit(solution)/shard_map/ppermute | solution.py:248
  36.2 0.3 collective-permute-done.4
  36.5 5.9 %collective-permute-done.3 = f16[4,128,128]{2,1,0:T(8,128)(2,1)S(1)} collective-permute-done((f16[4,128,128]{2,1,0:T(8,128)(2,1)S(1)}, f16[4,128,128]{2,1,0:T(8,128)(2,1)S(1)}, u32[]{:S(2)}, u32[]{:S(2)}) %collective-permute-start.3) | collective-permute-done | bytes 131104 | tf_op jit(solution)/shard_map/ppermute | solution.py:248
  42.4 0.0 collective-permute-done.5
  42.4 0.1 fusion.3.rows_ref
  42.4 0.6 %regroup.1 = f32[8,4,32,128]{3,2,1,0:T(8,128)S(1)} custom-call(s32[8]{0:T(128)S(1)} %copy-done.4, f32[4,128,128]{2,1,0:T(8,128)S(1)} %fusion.3.rows_ref), custom_call_target="tpu_custom_call" | custom-call | tf_op jit(solution)/shard_map/regroup/pallas_call | solution.py:226
  43.0 0.8 %multiply_convert_fusion = f16[8,4,32,128]{3,2,1,0:T(8,128)(2,1)} fusion(f32[8,4,32,128]{3,2,1,0:T(8,128)S(1)} %regroup.1), kind=kLoop, calls=%fused_computation.3 | loop fusion | flops 262144 | bytes 786432 | tf_op jit(solution)/shard_map/convert_element_type | solution.py:274
  43.8 4.5 %all-to-all-start = ((f16[8,4,32,128]{3,2,1,0:T(8,128)(2,1)}), f16[8,4,32,128]{3,2,1,0:T(8,128)(2,1)S(1)}, u32[]{:S(2)}, u32[]{:S(2)}) async-start(f16[8,4,32,128]{3,2,1,0:T(8,128)(2,1)} %multiply_convert_fusion), calls=%async_computation | async-start | bytes 524288 | tf_op jit(solution)/shard_map/all_to_all | solution.py:274
  48.3 0.6 %dynamic_slice.3 = s32[1]{0:T(128)} dynamic-slice(s32[8]{0:T(128)S(1)} %copy-done.4, s32[]{:T(128)S(6)} %select_n.7), dynamic_slice_sizes={1} | dynamic-slice | bytes 12 | tf_op jit(solution)/shard_map/dynamic_slice | solution.py:277
  48.9 0.6 %iota_compare_fusion = pred[32]{0:T(512)(128)(4,1)S(1)} fusion(s32[]{:T(128)} %bitcast), kind=kLoop, calls=%fused_computation.15 | loop fusion | flops 32 | bytes 36 | tf_op jit(solution)/shard_map/lt | solution.py:277
  49.6 0.5 slice.28
  50.8 5.8 %all-to-all-done = f16[8,4,32,128]{3,2,1,0:T(8,128)(2,1)S(1)} async-done(((f16[8,4,32,128]{3,2,1,0:T(8,128)(2,1)}), f16[8,4,32,128]{3,2,1,0:T(8,128)(2,1)S(1)}, u32[]{:S(2)}, u32[]{:S(2)}) %all-to-all-start) | async-done | bytes 262176 | tf_op jit(solution)/shard_map/all_to_all | solution.py:274
  56.6 0.1 convert_multiply_fusion
  56.6 1.1 %fusion = f32[1,32,32,128]{3,2,1,0:T(8,128)} fusion(f32[32,32,128]{2,1,0:T(8,128)S(1)} %bitcast.23, pred[32]{0:T(512)(128)(4,1)S(1)} %iota_compare_fusion), kind=kLoop, calls=%fused_computation.1 | loop fusion | flops 131072 | bytes 1048608 | tf_op jit(solution)/shard_map/broadcast_in_dim | solution.py:279
  (11 shorter events, 0.1 us)
Async XLA Ops:
  0.0 14.5 %copy-start.1 = (s32[64,64]{1,0:T(8,128)S(1)}, s32[64,64]{1,0:T(8,128)}, u32[]{:S(2)}) copy-start(s32[64,64]{1,0:T(8,128)} %segment_ref.5) | copy-start | bytes 49156
  0.0 14.5 %copy-start.2 = (s32[64,64]{1,0:T(8,128)S(1)}, s32[64,64]{1,0:T(8,128)}, u32[]{:S(2)}) copy-start(s32[64,64]{1,0:T(8,128)} %tile_ref.5) | copy-start | bytes 49156
  0.0 14.5 %copy-start.3 = (s32[64]{0:T(128)S(1)}, s32[64]{0:T(128)}, u32[]{:S(2)}) copy-start(s32[64]{0:T(128)} %order_ref.5) | copy-start | bytes 772
  0.0 14.5 %copy-start = (bf16[16,128,128]{2,1,0:T(8,128)(2,1)S(1)}, bf16[16,128,128]{2,1,0:T(8,128)(2,1)}, u32[]{:S(2)}) copy-start(bf16[16,128,128]{2,1,0:T(8,128)(2,1)} %tiles_ref.5) | copy-start | bytes 1572868
  10.0 4.5 %collective-permute-start = (bf16[4,16,128,128]{3,2,1,0:T(8,128)(2,1)S(1)}, bf16[4,16,128,128]{3,2,1,0:T(8,128)(2,1)}, u32[]{:S(2)}, u32[]{:S(2)}) collective-permute-start(bf16[4,16,128,128]{3,2,1,0:T(8,128)(2,1)S(1)} %paganin.1.refs_0_), channel_id=1, source_target_pairs={{0,1},{1,0},{2,3},{3,2},{4,5},{5,4},{6,7},{7,6},{8,9},{9,8},{10,11... | collective-permute-start | bytes 6291464 | tf_op jit(solution)/shard_map/ppermute | solution.py:254
  17.0 9.5 %collective-permute-start.1 = (f16[2,4,128,128]{3,2,1,0:T(8,128)(2,1)S(1)}, f16[2,4,128,128]{3,2,1,0:T(8,128)(2,1)S(1)}, u32[]{:S(2)}, u32[]{:S(2)}) collective-permute-start(f16[2,4,128,128]{3,2,1,0:T(8,128)(2,1)S(1)} %convert_element_type.36), channel_id=1, source_target_pairs={{0,2},{2,0},{4,6},{6,4},{8,10},{10,8},{12,14},{14,12},{1,3},{3,1},... | collective-permute-start | bytes 786440 | tf_op jit(solution)/shard_map/ppermute | solution.py:248
  26.5 15.9 %copy-start.4 = (s32[8]{0:T(128)S(1)}, s32[8]{0:T(128)}, u32[]{:S(2)}) copy-start(s32[8]{0:T(128)} %counts_ref.1) | copy-start | bytes 100
  26.6 7.8 %collective-permute-start.2 = (f16[2,4,128,128]{3,2,1,0:T(8,128)(2,1)S(1)}, f16[2,4,128,128]{3,2,1,0:T(8,128)(2,1)S(1)}, u32[]{:S(2)}, u32[]{:S(2)}) collective-permute-start(f16[2,4,128,128]{3,2,1,0:T(8,128)(2,1)S(1)} %convert_element_type.35), channel_id=1, source_target_pairs={{0,2},{2,0},{4,6},{6,4},{8,10},{10,8},{12,14},{14,12},{1,3},{3,1},... | collective-permute-start | bytes 786440 | tf_op jit(solution)/shard_map/ppermute | solution.py:248
  28.4 8.0 %collective-permute-start.4 = (f16[4,128,128]{2,1,0:T(8,128)(2,1)S(1)}, f16[4,128,128]{2,1,0:T(8,128)(2,1)S(1)}, u32[]{:S(2)}, u32[]{:S(2)}) collective-permute-start(f16[4,128,128]{2,1,0:T(8,128)(2,1)S(1)} %get-tuple-element.16), channel_id=1, source_target_pairs={{0,12},{2,14},{4,8},{6,10},{8,4},{10,6},{12,0},{14,2},{1,13},{3,15... | collective-permute-start | bytes 393224 | tf_op jit(solution)/shard_map/ppermute | solution.py:248
  32.2 10.2 %collective-permute-start.3 = (f16[4,128,128]{2,1,0:T(8,128)(2,1)S(1)}, f16[4,128,128]{2,1,0:T(8,128)(2,1)S(1)}, u32[]{:S(2)}, u32[]{:S(2)}) collective-permute-start(f16[4,128,128]{2,1,0:T(8,128)(2,1)S(1)} %get-tuple-element.15), channel_id=1, source_target_pairs={{0,8},{2,10},{4,12},{6,14},{8,0},{10,2},{12,4},{14,6},{1,9},{3,11}... | collective-permute-start | bytes 393224 | tf_op jit(solution)/shard_map/ppermute | solution.py:248
  34.5 7.8 %collective-permute-start.5 = (f16[4,128,128]{2,1,0:T(8,128)(2,1)S(1)}, f16[4,128,128]{2,1,0:T(8,128)(2,1)S(1)}, u32[]{:S(2)}, u32[]{:S(2)}) collective-permute-start(f16[4,128,128]{2,1,0:T(8,128)(2,1)S(1)} %fusion.4), channel_id=1, source_target_pairs={{0,4},{2,6},{4,0},{6,2},{8,12},{10,14},{12,8},{14,10},{1,5},{3,7},... | collective-permute-start | bytes 393224 | tf_op jit(solution)/shard_map/ppermute | solution.py:248
  43.8 12.7 %all-to-all-start = ((f16[8,4,32,128]{3,2,1,0:T(8,128)(2,1)}), f16[8,4,32,128]{3,2,1,0:T(8,128)(2,1)S(1)}, u32[]{:S(2)}, u32[]{:S(2)}) async-start(f16[8,4,32,128]{3,2,1,0:T(8,128)(2,1)} %multiply_convert_fusion), calls=%async_computation | async-start | bytes 524288 | tf_op jit(solution)/shard_map/all_to_all | solution.py:274

commit v5 on v4

--- a/solution.py
+++ b/solution.py
@@ -14,7 +14,7 @@
 sublanes = 8
 strands = 16
 chunks = strands * sublanes
-pitch_pad = 8
+pitch_pad = 1
 kernel_vmem = 24 << 20
 thickness_bound = 1.75
 send_bound = 60000.0
@@ -47,7 +47,11 @@
     levels = chunks.bit_length() - 1
     powers = [root] + [root ** (chunk << s) for s in range(levels)]
     powers.append(1.0 / (1.0 - root ** (chunk * chunks)))
-    powers = np.repeat(np.stack(powers), sublanes, axis=0).astype(np.float32)
+    powers = np.repeat(np.stack(powers), sublanes, axis=0)
+    step = np.arange(chunk)[:, None]
+    ahead = root ** (step + 1) * (1.0 - root ** (2 * (chunk - step))) / (1.0 - root * root)
+    behind = root ** (chunk - step)
+    powers = np.concatenate([ahead, behind, powers], axis=0).astype(np.float32)
     back = hartley * (root / paganin_alpha)[None, :]
     return paired_table(hartley, 0), paired_table(back, 1), jnp.asarray(powers)
 
@@ -60,17 +64,19 @@
     return moved
 
 
-def carries(ends, powers_ref, direction):
+def carries(ends, powers_ref, first, direction):
     levels = chunks.bit_length() - 1
     for s in range(levels):
-        power = powers_ref[pl.ds((1 + s) * sublanes, sublanes), :]
+        power = powers_ref[pl.ds(first + s * sublanes, sublanes), :]
         before = chunk_shift(ends, direction << s)
         ends = [end + power * other for end, other in zip(ends, before)]
-    whole = powers_ref[pl.ds((1 + levels) * sublanes, sublanes), :]
+    whole = powers_ref[pl.ds(first + levels * sublanes, sublanes), :]
     return [whole * other for other in chunk_shift(ends, direction)]
 
 
-def filter_kernel(forward_ref, back_ref, powers_ref, f_ref, out_ref, modes_ref):
+def filter_kernel(
+    forward_ref, back_ref, powers_ref, f_ref, out_ref, modes_ref, enter_ref, return_ref
+):
     row_total, width = f_ref.shape[1:]
     edge = out_ref.shape[3]
     span = width // sublanes
@@ -86,29 +92,46 @@
             paired_parts(jnp.concatenate(turned, axis=0)), forward_ref[...], preferred_element_type=jnp.float32
         )
 
-    root = powers_ref[pl.ds(0, sublanes), :]
+    root = powers_ref[pl.ds(2 * chunk, sublanes), :]
+    first = 2 * chunk + sublanes
 
     def strand(q, step):
         return pl.ds(q * chunk + step, sublanes, stride=pitch)
 
-    def sweep(values, order, keep):
+    def sweep(order):
+        values = [jnp.zeros((sublanes, row_total), jnp.float32)] * strands
         for step in order:
             for q in range(strands):
                 values[q] = modes_ref[strand(q, step), :] + root * values[q]
-                if keep:
-                    modes_ref[strand(q, step), :] = values[q]
+                modes_ref[strand(q, step), :] = values[q]
         return values
 
-    for direction in (1, -1):
-        order = range(chunk)[::direction]
-        zeros = [jnp.zeros((sublanes, row_total), jnp.float32)] * strands
-        ends = sweep(zeros, order, False)
-        sweep(carries(ends, powers_ref, direction), order, True)
+    ends = sweep(range(chunk))
+    firsts = sweep(range(chunk)[::-1])
+    entering = carries(ends, powers_ref, first, 1)
+    head = powers_ref[pl.ds(0, 1), :]
+    firsts = [value + head * enter for value, enter in zip(firsts, entering)]
+    returning = carries(firsts, powers_ref, first, -1)
+    for q in range(strands):
+        enter_ref[pl.ds(q, sublanes, stride=strands + pitch_pad), :] = entering[q]
+        return_ref[pl.ds(q, sublanes, stride=strands + pitch_pad), :] = returning[q]
+
+    def solved(column):
+        pieces = []
+        for start in range(column, column + span, chunk):
+            rows = modes_ref[pl.ds(place(start), chunk), :]
+            number = start // chunk + start // span * pitch_pad
+            pieces.append(
+                rows
+                + powers_ref[pl.ds(0, chunk), :] * enter_ref[pl.ds(number, 1), :]
+                + powers_ref[pl.ds(chunk, chunk), :] * return_ref[pl.ds(number, 1), :]
+            )
+        return jnp.concatenate(pieces, axis=0)
 
     for column in range(0, width, span):
         filtered = lax.dot_general(
             back_ref[...],
-            paired_parts(modes_ref[pl.ds(place(column), span), :]),
+            paired_parts(solved(column)),
             (((1,), (1,)), ((), ())),
             preferred_element_type=jnp.float32,
         )
@@ -134,7 +157,11 @@
         ],
         out_specs=pl.BlockSpec((1, segments, row_total, voxel_edge), lambda a: (a, 0, 0, 0)),
         out_shape=jax.ShapeDtypeStruct((angle_count, segments, row_total, voxel_edge), jnp.bfloat16),
-        scratch_shapes=[pltpu.VMEM((width + sublanes * pitch_pad, row_total), jnp.float32)],
+        scratch_shapes=[
+            pltpu.VMEM((width + sublanes * pitch_pad, row_total), jnp.float32),
+            pltpu.VMEM((chunks + sublanes * pitch_pad, row_total), jnp.float32),
+            pltpu.VMEM((chunks + sublanes * pitch_pad, row_total), jnp.float32),
+        ],
         compiler_params=pltpu.CompilerParams(vmem_limit_bytes=kernel_vmem),
         name="paganin",
     )(*[pltpu.with_memory_space_constraint(v, pltpu.HBM) for v in (forward, back, powers, intensity)])

time: 58.1 us -> 55.8 us (0.960)
  Pallas kernels: 19.2 us -> 16.9 us
    pallas_call x1, Pallas kernels: 10 us -> 7.74 us  [paganin_thickness(): pl.pallas_call(filter_kernel, grid=(angle_count,), in_specs=[pl.BlockSpec...]
where the time goes in v5:
time: 55.8 us; the launch traced here: 55.5 us
  waiting for transfers between devices  18.5 us (33%)
  Pallas kernels  16.9 us (30%)
  starting transfers between devices  15.1 us (27%)
  other arithmetic  2.99 us (5%)
  local copies, waits for them, and re-layouts  1.21 us (2%)
  between operations  0.74 us (1%)
    ppermute x5, starting transfers between devices, swap(): lax.ppermute(values, 'angle', [(i, i ^ partner) for i in range(group_tota...  10 us
    ppermute x5, waiting for transfers between devices, swap(): lax.ppermute(values, 'angle', [(i, i ^ partner) for i in range(group_tota...  8.83 us
    pallas_call x3, Pallas kernels, backproject(): pl.pallas_call(functools.partial(backproject_kernel, tuple(partners)), in...  8.6 us
    pallas_call x1, Pallas kernels, paganin_thickness(): pl.pallas_call(filter_kernel, grid=(angle_count,), in_specs=[pl.BlockSpec...  7.74 us
    all_to_all x1, waiting for transfers between devices, per_device(): lax.all_to_all(slots.astype(jnp.float16), 'angle', split_axis=0, concat_a...  5.8 us
    all_to_all x1, starting transfers between devices, per_device(): lax.all_to_all(slots.astype(jnp.float16), 'angle', split_axis=0, concat_a...  4.49 us
    ppermute x1, waiting for transfers between devices, per_device(): sources.append(lax.ppermute(thickness, 'tile', ring))  3.84 us
    broadcast_in_dim x1, other arithmetic, per_device(): return jnp.swapaxes(volume, 0, 1)[None]  1.13 us
  transfers between devices with their start and end apart: 7, of which 6 were waited for; matrix products, arithmetic and copies ran while one was open for 4% of the time, Pallas kernels for 11%

profile of v5, /device:TPU:0, one launch (start us, length us, event | category | flops | bytes accessed | tf_op | source)
XLA Modules:
  0.0 55.5 jit_solution(16780187599221507750)
XLA Ops:
  0.0 7.7 %paganin.1.refs_0_ = bf16[4,16,128,128]{3,2,1,0:T(8,128)(2,1)S(1)} custom-call(bf16[384,128]{1,0:T(8,128)(2,1)} %constant.27.clone.forward_ref, bf16[128,384]{1,0:T(8,128)(2,1)} %constant.28.clone.back_ref, f32[104,128]{1,0:T(8,128)} %constant.29.clone.powers_ref, f32[4,128,2048]{2,1,0:T(8,128)} %f_ref.1), custom_call_target="tpu_custom_call" | custom-call | tf_op jit(solution)/shard_map/paganin/pallas_call | solution.py:149
  7.8 0.6 %collective-permute-start = (bf16[4,16,128,128]{3,2,1,0:T(8,128)(2,1)S(1)}, bf16[4,16,128,128]{3,2,1,0:T(8,128)(2,1)}, u32[]{:S(2)}, u32[]{:S(2)}) collective-permute-start(bf16[4,16,128,128]{3,2,1,0:T(8,128)(2,1)S(1)} %paganin.1.refs_0_), channel_id=1, source_target_pairs={{0,1},{1,0},{2,3},{3,2},{4,5},{5,4},{6,7},{7,6},{8,9},{9,8},{10,11... | collective-permute-start | bytes 6291464 | tf_op jit(solution)/shard_map/ppermute | solution.py:281
  8.4 0.1 pad_add_fusion.place_ref
  8.4 3.8 %collective-permute-done.refs_1_ = bf16[4,16,128,128]{3,2,1,0:T(8,128)(2,1)} collective-permute-done((bf16[4,16,128,128]{3,2,1,0:T(8,128)(2,1)S(1)}, bf16[4,16,128,128]{3,2,1,0:T(8,128)(2,1)}, u32[]{:S(2)}, u32[]{:S(2)}) %collective-permute-start) | collective-permute-done | bytes 2097184 | tf_op jit(solution)/shard_map/ppermute | solution.py:281
  12.3 0.0 copy-done.1
  12.3 0.0 copy-done.2
  12.3 2.4 %backproject.5 = (f32[2,4,128,128]{3,2,1,0:T(8,128)S(1)}, f32[8,128]{1,0:T(8,128)S(1)}) custom-call(s32[3]{0:T(128)S(1)} %pad_add_fusion.place_ref, s32[64,64]{1,0:T(8,128)S(1)} %copy-done.1, s32[64,64]{1,0:T(8,128)S(1)} %copy-done.2, s32[64]{0:T(128)S(1)} %copy-done.3, bf16[16,128,128]{2,1,0:T(8,128)(2,1)S(1)} %copy-done, ...), custom_call_target="tpu_custom_call" | custom-call | flops 268435456 | bytes 524288 | tf_op jit(solution)/shard_map/backproject/pallas_call | solution.py:220
  14.7 2.9 %collective-permute-start.1 = (f16[2,4,128,128]{3,2,1,0:T(8,128)(2,1)S(1)}, f16[2,4,128,128]{3,2,1,0:T(8,128)(2,1)S(1)}, u32[]{:S(2)}, u32[]{:S(2)}) collective-permute-start(f16[2,4,128,128]{3,2,1,0:T(8,128)(2,1)S(1)} %convert_element_type.36), channel_id=1, source_target_pairs={{0,2},{2,0},{4,6},{6,4},{8,10},{10,8},{12,14},{14,12},{1,3},{3,1},... | collective-permute-start | bytes 786440 | tf_op jit(solution)/shard_map/ppermute | solution.py:275
  17.6 2.8 %backproject.4 = (f32[2,4,128,128]{3,2,1,0:T(8,128)S(1)}, f32[8,128]{1,0:T(8,128)}) custom-call(s32[3]{0:T(128)S(1)} %pad_add_fusion.place_ref, s32[64,64]{1,0:T(8,128)S(1)} %copy-done.1, s32[64,64]{1,0:T(8,128)S(1)} %copy-done.2, s32[64]{0:T(128)S(1)} %copy-done.3, bf16[16,128,128]{2,1,0:T(8,128)(2,1)S(1)} %copy-done, ...), custom_call_target="tpu_custom_call" | custom-call | flops 268435456 | bytes 524288 | tf_op jit(solution)/shard_map/backproject/pallas_call | solution.py:220
  20.5 3.4 %backproject.3 = (f32[4,4,128,128]{3,2,1,0:T(8,128)S(1)}, f32[8,128]{1,0:T(8,128)}) custom-call(s32[3]{0:T(128)S(1)} %pad_add_fusion.place_ref, s32[64,64]{1,0:T(8,128)S(1)} %copy-done.1, s32[64,64]{1,0:T(8,128)S(1)} %copy-done.2, s32[64]{0:T(128)S(1)} %copy-done.3, bf16[16,128,128]{2,1,0:T(8,128)(2,1)S(1)} %copy-done, ...), custom_call_target="tpu_custom_call" | custom-call | flops 536870912 | bytes 1048576 | tf_op jit(solution)/shard_map/backproject/pallas_call | solution.py:220
  23.9 0.3 collective-permute-done.1
  24.2 0.1 add_convert_fusion
  24.3 1.8 %collective-permute-start.2 = (f16[2,4,128,128]{3,2,1,0:T(8,128)(2,1)S(1)}, f16[2,4,128,128]{3,2,1,0:T(8,128)(2,1)S(1)}, u32[]{:S(2)}, u32[]{:S(2)}) collective-permute-start(f16[2,4,128,128]{3,2,1,0:T(8,128)(2,1)S(1)} %convert_element_type.35), channel_id=1, source_target_pairs={{0,2},{2,0},{4,6},{6,4},{8,10},{10,8},{12,14},{14,12},{1,3},{3,1},... | collective-permute-start | bytes 786440 | tf_op jit(solution)/shard_map/ppermute | solution.py:275
  26.1 0.1 slice_bitcast_fusion.2
  26.2 3.7 %collective-permute-start.4 = (f16[4,128,128]{2,1,0:T(8,128)(2,1)S(1)}, f16[4,128,128]{2,1,0:T(8,128)(2,1)S(1)}, u32[]{:S(2)}, u32[]{:S(2)}) collective-permute-start(f16[4,128,128]{2,1,0:T(8,128)(2,1)S(1)} %get-tuple-element.16), channel_id=1, source_target_pairs={{0,12},{2,14},{4,8},{6,10},{8,4},{10,6},{12,0},{14,2},{1,13},{3,15... | collective-permute-start | bytes 393224 | tf_op jit(solution)/shard_map/ppermute | solution.py:275
  29.9 0.0 collective-permute-start.3
  29.9 2.3 %collective-permute-done.2 = f16[2,4,128,128]{3,2,1,0:T(8,128)(2,1)S(1)} collective-permute-done((f16[2,4,128,128]{3,2,1,0:T(8,128)(2,1)S(1)}, f16[2,4,128,128]{3,2,1,0:T(8,128)(2,1)S(1)}, u32[]{:S(2)}, u32[]{:S(2)}) %collective-permute-start.2) | collective-permute-done | bytes 262176 | tf_op jit(solution)/shard_map/ppermute | solution.py:275
  32.2 0.1 convert_add_fusion
  32.3 1.6 %collective-permute-start.5 = (f16[4,128,128]{2,1,0:T(8,128)(2,1)S(1)}, f16[4,128,128]{2,1,0:T(8,128)(2,1)S(1)}, u32[]{:S(2)}, u32[]{:S(2)}) collective-permute-start(f16[4,128,128]{2,1,0:T(8,128)(2,1)S(1)} %fusion.4), channel_id=1, source_target_pairs={{0,4},{2,6},{4,0},{6,2},{8,12},{10,14},{12,8},{14,10},{1,5},{3,7},... | collective-permute-start | bytes 393224 | tf_op jit(solution)/shard_map/ppermute | solution.py:275
  33.9 0.2 collective-permute-done.4
  34.1 6.1 %collective-permute-done.3 = f16[4,128,128]{2,1,0:T(8,128)(2,1)S(1)} collective-permute-done((f16[4,128,128]{2,1,0:T(8,128)(2,1)S(1)}, f16[4,128,128]{2,1,0:T(8,128)(2,1)S(1)}, u32[]{:S(2)}, u32[]{:S(2)}) %collective-permute-start.3) | collective-permute-done | bytes 131104 | tf_op jit(solution)/shard_map/ppermute | solution.py:275
  40.1 0.0 collective-permute-done.5
  40.1 0.1 fusion.3.rows_ref
  40.2 0.6 %regroup.1 = f32[8,4,32,128]{3,2,1,0:T(8,128)S(1)} custom-call(s32[8]{0:T(128)S(1)} %copy-done.4, f32[4,128,128]{2,1,0:T(8,128)S(1)} %fusion.3.rows_ref), custom_call_target="tpu_custom_call" | custom-call | tf_op jit(solution)/shard_map/regroup/pallas_call | solution.py:253
  40.8 0.8 %multiply_convert_fusion = f16[8,4,32,128]{3,2,1,0:T(8,128)(2,1)} fusion(f32[8,4,32,128]{3,2,1,0:T(8,128)S(1)} %regroup.1), kind=kLoop, calls=%fused_computation.3 | loop fusion | flops 262144 | bytes 786432 | tf_op jit(solution)/shard_map/convert_element_type | solution.py:301
  41.6 4.5 %all-to-all-start = ((f16[8,4,32,128]{3,2,1,0:T(8,128)(2,1)}), f16[8,4,32,128]{3,2,1,0:T(8,128)(2,1)S(1)}, u32[]{:S(2)}, u32[]{:S(2)}) async-start(f16[8,4,32,128]{3,2,1,0:T(8,128)(2,1)} %multiply_convert_fusion), calls=%async_computation | async-start | bytes 524288 | tf_op jit(solution)/shard_map/all_to_all | solution.py:301
  46.1 0.6 %dynamic_slice.3 = s32[1]{0:T(128)} dynamic-slice(s32[8]{0:T(128)S(1)} %copy-done.4, s32[]{:T(128)S(6)} %select_n.7), dynamic_slice_sizes={1} | dynamic-slice | bytes 12 | tf_op jit(solution)/shard_map/dynamic_slice | solution.py:304
  46.7 0.6 %iota_compare_fusion = pred[32]{0:T(512)(128)(4,1)S(1)} fusion(s32[]{:T(128)} %bitcast), kind=kLoop, calls=%fused_computation.15 | loop fusion | flops 32 | bytes 36 | tf_op jit(solution)/shard_map/lt | solution.py:304
  47.3 0.5 slice.28
  48.5 5.8 %all-to-all-done = f16[8,4,32,128]{3,2,1,0:T(8,128)(2,1)S(1)} async-done(((f16[8,4,32,128]{3,2,1,0:T(8,128)(2,1)}), f16[8,4,32,128]{3,2,1,0:T(8,128)(2,1)S(1)}, u32[]{:S(2)}, u32[]{:S(2)}) %all-to-all-start) | async-done | bytes 262176 | tf_op jit(solution)/shard_map/all_to_all | solution.py:301
  54.3 0.1 convert_multiply_fusion
  54.3 1.1 %fusion = f32[1,32,32,128]{3,2,1,0:T(8,128)} fusion(f32[32,32,128]{2,1,0:T(8,128)S(1)} %bitcast.23, pred[32]{0:T(512)(128)(4,1)S(1)} %iota_compare_fusion), kind=kLoop, calls=%fused_computation.1 | loop fusion | flops 131072 | bytes 1048608 | tf_op jit(solution)/shard_map/broadcast_in_dim | solution.py:306
  (11 shorter events, 0.1 us)
Async XLA Ops:
  0.0 12.3 %copy-start.1 = (s32[64,64]{1,0:T(8,128)S(1)}, s32[64,64]{1,0:T(8,128)}, u32[]{:S(2)}) copy-start(s32[64,64]{1,0:T(8,128)} %segment_ref.5) | copy-start | bytes 49156
  0.0 12.3 %copy-start.2 = (s32[64,64]{1,0:T(8,128)S(1)}, s32[64,64]{1,0:T(8,128)}, u32[]{:S(2)}) copy-start(s32[64,64]{1,0:T(8,128)} %tile_ref.5) | copy-start | bytes 49156
  0.0 12.3 %copy-start.3 = (s32[64]{0:T(128)S(1)}, s32[64]{0:T(128)}, u32[]{:S(2)}) copy-start(s32[64]{0:T(128)} %order_ref.5) | copy-start | bytes 772
  0.0 12.3 %copy-start = (bf16[16,128,128]{2,1,0:T(8,128)(2,1)S(1)}, bf16[16,128,128]{2,1,0:T(8,128)(2,1)}, u32[]{:S(2)}) copy-start(bf16[16,128,128]{2,1,0:T(8,128)(2,1)} %tiles_ref.5) | copy-start | bytes 1572868
  7.8 4.5 %collective-permute-start = (bf16[4,16,128,128]{3,2,1,0:T(8,128)(2,1)S(1)}, bf16[4,16,128,128]{3,2,1,0:T(8,128)(2,1)}, u32[]{:S(2)}, u32[]{:S(2)}) collective-permute-start(bf16[4,16,128,128]{3,2,1,0:T(8,128)(2,1)S(1)} %paganin.1.refs_0_), channel_id=1, source_target_pairs={{0,1},{1,0},{2,3},{3,2},{4,5},{5,4},{6,7},{7,6},{8,9},{9,8},{10,11... | collective-permute-start | bytes 6291464 | tf_op jit(solution)/shard_map/ppermute | solution.py:281
  14.7 9.5 %collective-permute-start.1 = (f16[2,4,128,128]{3,2,1,0:T(8,128)(2,1)S(1)}, f16[2,4,128,128]{3,2,1,0:T(8,128)(2,1)S(1)}, u32[]{:S(2)}, u32[]{:S(2)}) collective-permute-start(f16[2,4,128,128]{3,2,1,0:T(8,128)(2,1)S(1)} %convert_element_type.36), channel_id=1, source_target_pairs={{0,2},{2,0},{4,6},{6,4},{8,10},{10,8},{12,14},{14,12},{1,3},{3,1},... | collective-permute-start | bytes 786440 | tf_op jit(solution)/shard_map/ppermute | solution.py:275
  24.2 15.9 %copy-start.4 = (s32[8]{0:T(128)S(1)}, s32[8]{0:T(128)}, u32[]{:S(2)}) copy-start(s32[8]{0:T(128)} %counts_ref.1) | copy-start | bytes 100
  24.3 7.8 %collective-permute-start.2 = (f16[2,4,128,128]{3,2,1,0:T(8,128)(2,1)S(1)}, f16[2,4,128,128]{3,2,1,0:T(8,128)(2,1)S(1)}, u32[]{:S(2)}, u32[]{:S(2)}) collective-permute-start(f16[2,4,128,128]{3,2,1,0:T(8,128)(2,1)S(1)} %convert_element_type.35), channel_id=1, source_target_pairs={{0,2},{2,0},{4,6},{6,4},{8,10},{10,8},{12,14},{14,12},{1,3},{3,1},... | collective-permute-start | bytes 786440 | tf_op jit(solution)/shard_map/ppermute | solution.py:275
  26.2 7.9 %collective-permute-start.4 = (f16[4,128,128]{2,1,0:T(8,128)(2,1)S(1)}, f16[4,128,128]{2,1,0:T(8,128)(2,1)S(1)}, u32[]{:S(2)}, u32[]{:S(2)}) collective-permute-start(f16[4,128,128]{2,1,0:T(8,128)(2,1)S(1)} %get-tuple-element.16), channel_id=1, source_target_pairs={{0,12},{2,14},{4,8},{6,10},{8,4},{10,6},{12,0},{14,2},{1,13},{3,15... | collective-permute-start | bytes 393224 | tf_op jit(solution)/shard_map/ppermute | solution.py:275
  29.9 10.3 %collective-permute-start.3 = (f16[4,128,128]{2,1,0:T(8,128)(2,1)S(1)}, f16[4,128,128]{2,1,0:T(8,128)(2,1)S(1)}, u32[]{:S(2)}, u32[]{:S(2)}) collective-permute-start(f16[4,128,128]{2,1,0:T(8,128)(2,1)S(1)} %get-tuple-element.15), channel_id=1, source_target_pairs={{0,8},{2,10},{4,12},{6,14},{8,0},{10,2},{12,4},{14,6},{1,9},{3,11}... | collective-permute-start | bytes 393224 | tf_op jit(solution)/shard_map/ppermute | solution.py:275
  32.3 7.8 %collective-permute-start.5 = (f16[4,128,128]{2,1,0:T(8,128)(2,1)S(1)}, f16[4,128,128]{2,1,0:T(8,128)(2,1)S(1)}, u32[]{:S(2)}, u32[]{:S(2)}) collective-permute-start(f16[4,128,128]{2,1,0:T(8,128)(2,1)S(1)} %fusion.4), channel_id=1, source_target_pairs={{0,4},{2,6},{4,0},{6,2},{8,12},{10,14},{12,8},{14,10},{1,5},{3,7},... | collective-permute-start | bytes 393224 | tf_op jit(solution)/shard_map/ppermute | solution.py:275
  41.6 12.7 %all-to-all-start = ((f16[8,4,32,128]{3,2,1,0:T(8,128)(2,1)}), f16[8,4,32,128]{3,2,1,0:T(8,128)(2,1)S(1)}, u32[]{:S(2)}, u32[]{:S(2)}) async-start(f16[8,4,32,128]{3,2,1,0:T(8,128)(2,1)} %multiply_convert_fusion), calls=%async_computation | async-start | bytes 524288 | tf_op jit(solution)/shard_map/all_to_all | solution.py:301
